TPU v7x, 32 devices: a whole 2x2x4 slice. The times are simulated.
32 devices in a mesh: wide: 8 (over z, y), narrow: 4 (over x, core).
Axes of the slice: x: 2, y: 2, z: 4, core: 2. Of those that a mesh axis runs over, the one named last changes fastest.
Arguments:
- inputs: bfloat16 [4, 1024, 1536], P('narrow', 'wide'), may hold values from -6 to 6
- out_grad: bfloat16 [4, 1024, 1536], P('narrow', 'wide'), may hold values from -6 to 6
- qkv_w: float32 [3, 1536, 1536], P(None, ('wide', 'narrow')), may hold values from -0.15625 to 0.15625
- out_w: float32 [1536, 1536], P(('wide', 'narrow')), may hold values from -0.875 to 0.875
- ffn_in: float32 [2, 1536, 4096], P(None, None, ('wide', 'narrow')), may hold values from -0.15625 to 0.15625
- ffn_out: float32 [4096, 1536], P(('wide', 'narrow')), may hold values from -0.09375 to 0.09375
- qkv_mom: float32 [3, 1536, 1536], P(None, ('wide', 'narrow')), may hold values from -0.0012207031 to 0.0012207031
- out_mom: float32 [1536, 1536], P(('wide', 'narrow')), may hold values from -0.0012207031 to 0.0012207031
- in_mom: float32 [2, 1536, 4096], P(None, None, ('wide', 'narrow')), may hold values from -0.0012207031 to 0.0012207031
- down_mom: float32 [4096, 1536], P(('wide', 'narrow')), may hold values from -0.0012207031 to 0.0012207031
- gains: float32 [2, 1536], replicated, may hold values from 0.5 to 1.5
- gains_m: float32 [2, 1536], replicated, may hold values from -0.00048828125 to 0.00048828125
- gains_v: float32 [2, 1536], replicated, may hold values from 1.4108595e-08 to 2.469004e-07
- fgate_w: float32 [1536, 24], replicated, may hold values from -0.15625 to 0.15625
- fgate_w_m: float32 [1536, 24], replicated, may hold values from -0.00012207031 to 0.00012207031
- fgate_w_v: float32 [1536, 24], replicated, may hold values from 9.1705865e-10 to 1.4814025e-08
- fgate_b: float32 [24], replicated, may hold values from 3 to 10
- fgate_b_m: float32 [24], replicated, may hold values from -0.0012207031 to 0.0012207031
- fgate_b_v: float32 [24], replicated, may hold values from 9.1705864e-08 to 1.4814025e-06
- doc_ids: int32 [4, 1024], P('narrow'), may hold values from 0 to 2, never falling along the last dimension, each value on 1 to 512 neighbouring positions
- group_ids: int32 [4, 16], P('narrow'), may hold values from 0 to 15, as said below
- block_mask: int32 [4, 16, 16], P('narrow'), may hold values 0 or 1
Outputs:
- output: bfloat16 [4, 1024, 1536], P('narrow', 'wide')
- grad_inputs: float32 [4, 1024, 1536], P('narrow', 'wide')
- grad_norm: float32 [1], replicated
- new_qkv_w: float32 [3, 1536, 1536], P(None, ('wide', 'narrow'))
- new_out_w: float32 [1536, 1536], P(('wide', 'narrow'))
- new_ffn_in: float32 [2, 1536, 4096], P(None, None, ('wide', 'narrow'))
- new_ffn_out: float32 [4096, 1536], P(('wide', 'narrow'))
- new_qkv_mom: float32 [3, 1536, 1536], P(None, ('wide', 'narrow'))
- new_out_mom: float32 [1536, 1536], P(('wide', 'narrow'))
- new_in_mom: float32 [2, 1536, 4096], P(None, None, ('wide', 'narrow'))
- new_down_mom: float32 [4096, 1536], P(('wide', 'narrow'))
- new_gains: float32 [2, 1536], replicated
- new_gains_m: float32 [2, 1536], replicated
- new_gains_v: float32 [2, 1536], replicated
- new_fgate_w: float32 [1536, 24], replicated
- new_fgate_w_m: float32 [1536, 24], replicated
- new_fgate_w_v: float32 [1536, 24], replicated
- new_fgate_b: float32 [24], replicated
- new_fgate_b_m: float32 [24], replicated
- new_fgate_b_v: float32 [24], replicated
Inputs may be any that keep to these rules, and one draw needn't show every extreme that they name: `group_ids`: in every sequence, slots 2w and 2w + 1 hold groups p(w) and 15 - p(w) for a permutation p of 0 to 7; every group is held once.
All inputs are finite; a program needn't handle non-finite values. No bound on the sum of `block_mask` on one device may be relied on, other than what follows from the above.
Results may differ from a plain program's by a relative error of at most 0.028.
Values may be sent and summed in bfloat16 or wider, within the bound.
No kernel may reach another device: no remote copies, remote signals or barrier semaphores. Data moves between devices by JAX's collectives and lax.ppermute only.
A program may use at most 448 MiB of HBM per device.

v0:
```python
import math

import jax
import jax.numpy as jnp
from jax import lax
from jax.sharding import PartitionSpec as P

D = 1536
H = 24
DH = 64
FF = 4096
SWEEPS = 5
STEP = 10
CH = 64


NORM_EPSILON = 1e-06
MASKED_SCORE = -1e30
COEF_LINEAR = 3.4445
COEF_CUBIC = -4.775
COEF_QUINTIC = 2.0315
MOMENTUM = 0.95
MUON_DECAY = 0.01
MUON_RATE = 0.5
BETA_FIRST = 0.9
BETA_SECOND = 0.95
ADAM_EPSILON = 1e-08
ADAM_DECAY = 0.1
RATE_GAINS = 1.0
RATE_FGATE_W = 0.03
RATE_FGATE_B = 4.0
CLIP_NORM = 1.0


def rms_parts(hidden):
    factor = lax.rsqrt(jnp.mean(hidden * hidden, axis=-1, keepdims=True) + NORM_EPSILON)
    return (hidden * factor, factor)


def rms_back(grad_normed, gain, normed, factor):
    scaled = grad_normed * gain
    return factor * (scaled - normed * jnp.mean(scaled * normed, axis=-1, keepdims=True))


def matmul_first(left, right):
    return lax.dot_general(
        left, right, (((0,), (0,)), ((), ())), preferred_element_type=jnp.float32
    )


def matmul_last(left, right):
    return lax.dot_general(
        left, right, (((1,), (1,)), ((), ())), preferred_element_type=jnp.float32
    )


def in_blocks(step_fn, running, portion, first_row):
    row_count = portion[0].shape[0]
    blocks = row_count // CH
    shaped = tuple((member.reshape((blocks, CH) + member.shape[1:]) for member in portion))

    def scan_step(status, element):
        offset, members = element
        return (step_fn(status, members, first_row + offset * CH), None)

    running, _ = lax.scan(scan_step, running, (jnp.arange(blocks), shaped))
    return running


def gather_pairs(keys_own, values_own):
    return (
        lax.all_gather(keys_own, "wide", axis=0, tiled=True),
        lax.all_gather(values_own, "wide", axis=0, tiled=True),
    )


def column_block(row_block, wide_rank, wide_count):
    width = row_block.shape[1] // wide_count
    return lax.dynamic_slice_in_dim(row_block, wide_rank * width, width, 1)


def adam_update(weight, first, second, gradient, bias_one, bias_two, step_rate):
    new_first = BETA_FIRST * first + (1.0 - BETA_FIRST) * gradient
    new_second = BETA_SECOND * second + (1.0 - BETA_SECOND) * gradient * gradient
    update = new_first / bias_one / (jnp.sqrt(new_second / bias_two) + ADAM_EPSILON)
    return (weight - step_rate * (update + ADAM_DECAY * weight), new_first, new_second)


def tall_rate(rows_count, cols_count, fan_in):
    return MUON_RATE * math.sqrt(max(rows_count, cols_count) / fan_in)


def shards(
    inputs,
    out_grad,
    qkv_w,
    out_w,
    ffn_in,
    ffn_out,
    qkv_mom,
    out_mom,
    in_mom,
    down_mom,
    gains,
    gains_m,
    gains_v,
    fgate_w,
    fgate_w_m,
    fgate_w_v,
    fgate_b,
    fgate_b_m,
    fgate_b_v,
    doc_ids,
    group_ids,
    block_mask,
):
    wide_rank = lax.axis_index("wide")
    wide_count = lax.axis_size("wide")
    tokens = inputs.shape[1]
    seq_len = doc_ids.shape[1]
    group_total = group_ids.shape[1]
    score_scale = DH ** (-0.5)
    full_qkv, full_out, full_in, full_down = (
        lax.all_gather(qkv_w.astype(jnp.bfloat16), ("wide", "narrow"), axis=1, tiled=True),
        lax.all_gather(out_w.astype(jnp.bfloat16), ("wide", "narrow"), axis=0, tiled=True),
        lax.all_gather(ffn_in.astype(jnp.bfloat16), ("wide", "narrow"), axis=2, tiled=True),
        lax.all_gather(ffn_out.astype(jnp.bfloat16), ("wide", "narrow"), axis=0, tiled=True),
    )
    w_qkv = full_qkv.transpose(1, 0, 2).reshape(D, 3 * D)
    w_gate_up = full_in.transpose(1, 0, 2).reshape(D, 2 * FF)
    w_forget = fgate_w.astype(jnp.bfloat16)
    within = jnp.arange(CH, dtype=jnp.int32)
    slot_ids = group_ids[0]
    own_ids = lax.dynamic_slice_in_dim(slot_ids, 2 * wide_rank, 2)
    pos_dev = (slot_ids[:, None] * CH + within[None, :]).reshape(seq_len)
    docs_seq = doc_ids[0]
    starts_seq = jnp.concatenate([jnp.ones((1,), jnp.bool_), docs_seq[1:] != docs_seq[:-1]])
    start_groups = starts_seq.reshape(group_total, CH)
    doc_dev = docs_seq[pos_dev]
    group_dev = jnp.repeat(slot_ids, CH)
    own_first = 2 * wide_rank * CH
    query_pos = lax.dynamic_slice_in_dim(pos_dev, own_first, tokens)
    query_doc = lax.dynamic_slice_in_dim(doc_dev, own_first, tokens)
    allow_pair = (own_ids[:, None] == jnp.arange(group_total)[None, :]) | (
        block_mask[0][own_ids] == 1
    )
    group_order = jnp.argsort(slot_ids)
    own_starts = start_groups[own_ids]
    resid_in = inputs[0].astype(jnp.float32)
    normed_one, factor_one = rms_parts(resid_in)
    attn_in = (normed_one * gains[0]).astype(jnp.bfloat16)
    projected = jnp.dot(attn_in, w_qkv, preferred_element_type=jnp.float32).astype(jnp.bfloat16)
    queries = projected[:, :D]
    keys_own = projected[:, D : 2 * D]
    values_own = projected[:, 2 * D :]
    queries3 = queries.reshape(tokens, H, DH)
    gate_logit = jnp.dot(attn_in, w_forget, preferred_element_type=jnp.float32) + fgate_b
    log_forget = jax.nn.log_sigmoid(gate_logit)
    forget_groups = log_forget.T.reshape(H, 2, CH)
    last_start = lax.cummax(jnp.where(own_starts, within[None, :], -1), axis=1)
    running = jnp.cumsum(forget_groups, axis=2)
    before = running - forget_groups
    base_index = jnp.broadcast_to(jnp.maximum(last_start, 0)[None], (H, 2, CH))
    segment_base = jnp.take_along_axis(before, base_index, axis=2) * (last_start >= 0)[None]
    local_cum = (running - segment_base).reshape(H, tokens)
    cum_all = lax.all_gather(local_cum, "wide", axis=1, tiled=True)
    cum_seq = cum_all.reshape(H, group_total, CH)[:, group_order, :]
    open_groups = (lax.cummax(jnp.where(start_groups, within[None, :], -1), axis=1) < 0).astype(
        jnp.float32
    )

    def carry_step(previous, element):
        last_cum, through = element
        return (last_cum + previous * through, previous)

    _, carries = lax.scan(
        carry_step, jnp.zeros((H,), jnp.float32), (cum_seq[:, :, -1].T, open_groups[:, -1])
    )
    cum_full = cum_seq + carries.T[:, :, None] * open_groups[None]
    cum_dev = cum_full[:, slot_ids, :].reshape(H, seq_len)
    query_cum = lax.dynamic_slice_in_dim(cum_dev, own_first, tokens, 1)

    def key_mask(first_row, row_count):
        key_pos = lax.dynamic_slice_in_dim(pos_dev, first_row, row_count)
        key_doc = lax.dynamic_slice_in_dim(doc_dev, first_row, row_count)
        key_group = lax.dynamic_slice_in_dim(group_dev, first_row, row_count)
        group_ok = jnp.take(allow_pair, key_group, axis=1)
        group_ok = jnp.broadcast_to(group_ok[:, None, :], (2, CH, row_count)).reshape(
            tokens, row_count
        )
        return (
            (key_pos[None, :] <= query_pos[:, None])
            & (key_doc[None, :] == query_doc[:, None])
            & group_ok
        )

    def block_scores(keyrows, first_row, row_count, allowed):
        key_cum = lax.dynamic_slice_in_dim(cum_dev, first_row, row_count, 1)
        raw = jnp.einsum("ihd,jhd->hij", queries3, keyrows, preferred_element_type=jnp.float32)
        scores = raw * score_scale + query_cum[:, :, None] - key_cum[:, None, :]
        return jnp.where(allowed[None], scores, MASKED_SCORE)

    def forward_step(status, portion, first_row):
        keyrows = portion[0].reshape(-1, H, DH)
        valrows = portion[1].reshape(-1, H, DH)
        row_count = keyrows.shape[0]
        allowed = key_mask(first_row, row_count)

        def update(current):
            top_old, total_old, acc_old = current
            scores = block_scores(keyrows, first_row, row_count, allowed)
            top_new = jnp.maximum(top_old, jnp.max(scores, axis=2))
            weights = jnp.where(allowed[None], jnp.exp(scores - top_new[:, :, None]), 0.0)
            rescale = jnp.exp(top_old - top_new)
            added = jnp.einsum(
                "hij,jhd->hid",
                weights.astype(jnp.bfloat16),
                valrows,
                preferred_element_type=jnp.float32,
            )
            return (
                top_new,
                total_old * rescale + jnp.sum(weights, axis=2),
                acc_old * rescale[:, :, None] + added,
            )

        return lax.cond(jnp.any(allowed), update, lambda current: current, status)

    start_state = (
        jnp.full((H, tokens), MASKED_SCORE, jnp.float32),
        jnp.zeros((H, tokens), jnp.float32),
        jnp.zeros((H, tokens, DH), jnp.float32),
    )
    top_all, total_all, acc_all = in_blocks(
        forward_step,
        start_state,
        (
            lax.all_gather(keys_own, "wide", axis=0, tiled=True),
            lax.all_gather(values_own, "wide", axis=0, tiled=True),
        ),
        jnp.int32(0),
    )
    log_total = top_all + jnp.log(total_all)
    attn_f32 = (acc_all / total_all[:, :, None]).transpose(1, 0, 2)
    attn_out = attn_f32.reshape(tokens, D).astype(jnp.bfloat16)
    middle = resid_in + jnp.dot(attn_out, full_out, preferred_element_type=jnp.float32)
    normed_two, factor_two = rms_parts(middle)
    ffn_input = (normed_two * gains[1]).astype(jnp.bfloat16)
    gate_up = jnp.dot(ffn_input, w_gate_up, preferred_element_type=jnp.float32)
    gate_value = gate_up[:, :FF]
    up_value = gate_up[:, FF:]
    gate_sigmoid = jax.nn.sigmoid(gate_value)
    hidden = (gate_value * gate_sigmoid * up_value).astype(jnp.bfloat16)
    result = middle + jnp.dot(hidden, full_down, preferred_element_type=jnp.float32)
    grad_out_b = out_grad[0]
    grad_out_f = grad_out_b.astype(jnp.float32)
    d_down = matmul_first(hidden, grad_out_b)
    grad_hidden = matmul_last(grad_out_b, full_down).astype(jnp.bfloat16).astype(jnp.float32)
    grad_gate = grad_hidden * up_value * gate_sigmoid * (1.0 + gate_value * (1.0 - gate_sigmoid))
    grad_up = grad_hidden * gate_value * gate_sigmoid
    grad_gate_up = jnp.concatenate([grad_gate, grad_up], axis=1).astype(jnp.bfloat16)
    d_gate_up = matmul_first(ffn_input, grad_gate_up).reshape(D, 2, FF).transpose(1, 0, 2)
    grad_normed_two = matmul_last(grad_gate_up, w_gate_up)
    d_gain_two = jnp.sum(grad_normed_two * normed_two, axis=0)
    grad_middle = grad_out_f + rms_back(grad_normed_two, gains[1], normed_two, factor_two)
    grad_branch = grad_middle.astype(jnp.bfloat16)
    d_out = matmul_first(attn_out, grad_branch)
    grad_attn = matmul_last(grad_branch, full_out).astype(jnp.bfloat16)
    grad_attn3 = grad_attn.reshape(tokens, H, DH)
    row_delta = jnp.sum(grad_attn3.astype(jnp.float32) * attn_f32, axis=2).T

    def score_grads(keyrows, valrows, first_row, row_count, allowed):
        scores = block_scores(keyrows, first_row, row_count, allowed)
        probs = jnp.exp(scores - log_total[:, :, None])
        dprobs = jnp.einsum("ihd,jhd->hij", grad_attn3, valrows, preferred_element_type=jnp.float32)
        return (probs, (probs * (dprobs - row_delta[:, :, None])).astype(jnp.bfloat16))

    def query_step(status, portion, first_row):
        keyrows = portion[0].reshape(-1, H, DH)
        valrows = portion[1].reshape(-1, H, DH)
        row_count = keyrows.shape[0]
        allowed = key_mask(first_row, row_count)

        def update(current):
            grad_old, cum_old = current
            _, dscores = score_grads(keyrows, valrows, first_row, row_count, allowed)
            added = (
                jnp.einsum("hij,jhd->hid", dscores, keyrows, preferred_element_type=jnp.float32)
                * score_scale
            )
            return (grad_old + added, cum_old + jnp.sum(dscores.astype(jnp.float32), axis=2))

        return lax.cond(jnp.any(allowed), update, lambda current: current, status)

    all_keys, all_values = gather_pairs(keys_own, values_own)
    grad_q_acc, cum_q_acc = in_blocks(
        query_step,
        (jnp.zeros((H, tokens, DH), jnp.float32), jnp.zeros((H, tokens), jnp.float32)),
        (all_keys, all_values),
        0,
    )
    query_stats = lax.all_gather(
        jnp.stack([log_total.T, row_delta.T, query_cum.T]), "wide", axis=1, tiled=True
    )
    own_keys3 = keys_own.reshape(tokens, H, DH)
    own_values3 = values_own.reshape(tokens, H, DH)
    own_group = lax.dynamic_slice_in_dim(group_dev, own_first, tokens)
    mask_table = block_mask[0] == 1

    def owner_step(status, portion, first_row):
        query_rows = portion[0].reshape(-1, H, DH)
        gradient_rows = portion[1].reshape(-1, H, DH)
        row_count = query_rows.shape[0]
        other_pos = lax.dynamic_slice_in_dim(pos_dev, first_row, row_count)
        other_doc = lax.dynamic_slice_in_dim(doc_dev, first_row, row_count)
        other_group = lax.dynamic_slice_in_dim(group_dev, first_row, row_count)
        group_ok = (other_group[:, None] == own_group[None, :]) | jnp.take(
            mask_table[other_group], own_group, axis=1
        )
        allowed = (
            (query_pos[None, :] <= other_pos[:, None])
            & (query_doc[None, :] == other_doc[:, None])
            & group_ok
        )
        stats = lax.dynamic_slice_in_dim(query_stats, first_row, row_count, 1)

        def update(current):
            keys_acc, values_acc, cum_acc = current
            raw = jnp.einsum(
                "ihd,jhd->hij", query_rows, own_keys3, preferred_element_type=jnp.float32
            )
            scores = raw * score_scale + stats[2].T[:, :, None] - query_cum[:, None, :]
            scores = jnp.where(allowed[None], scores, MASKED_SCORE)
            probs = jnp.exp(scores - stats[0].T[:, :, None])
            dprobs = jnp.einsum(
                "ihd,jhd->hij", gradient_rows, own_values3, preferred_element_type=jnp.float32
            )
            dscores = (probs * (dprobs - stats[1].T[:, :, None])).astype(jnp.bfloat16)
            keys_new = (
                keys_acc
                + jnp.einsum(
                    "hij,ihd->jhd", dscores, query_rows, preferred_element_type=jnp.float32
                )
                * score_scale
            )
            values_new = values_acc + jnp.einsum(
                "hij,ihd->jhd",
                probs.astype(jnp.bfloat16),
                gradient_rows,
                preferred_element_type=jnp.float32,
            )
            return (keys_new, values_new, cum_acc - jnp.sum(dscores.astype(jnp.float32), axis=1))

        return lax.cond(jnp.any(allowed), update, lambda current: current, status)

    owner_start = (
        jnp.zeros((tokens, H, DH), jnp.float32),
        jnp.zeros((tokens, H, DH), jnp.float32),
        jnp.zeros((H, tokens), jnp.float32),
    )
    keys_sum, values_sum, cum_sum = in_blocks(
        owner_step,
        owner_start,
        (
            lax.all_gather(queries, "wide", axis=0, tiled=True),
            lax.all_gather(grad_attn, "wide", axis=0, tiled=True),
        ),
        jnp.int32(0),
    )
    grad_keys = keys_sum.reshape(tokens, D)
    grad_values = values_sum.reshape(tokens, D)
    key_cum_grad = cum_sum.T
    cum_grad = (cum_q_acc + key_cum_grad.T).reshape(H, 2, CH)
    later_starts = jnp.where(own_starts & (within[None, :] > 0), within[None, :], CH)
    first_break = jnp.min(later_starts, axis=1)
    lead_part = jnp.sum(
        jnp.where(within[None, None, :] < first_break[None, :, None], cum_grad, 0.0), axis=2
    )
    lead_all = lax.all_gather(lead_part, "wide", axis=1, tiled=True)
    lead_seq = lead_all[:, group_order]
    through_seq = jnp.logical_not(jnp.any(start_groups[:, 1:], axis=1)).astype(jnp.float32)
    open_next = jnp.concatenate(
        [jnp.logical_not(start_groups[1:, 0]), jnp.zeros((1,), jnp.bool_)]
    ).astype(jnp.float32)

    def back_step(following, element):
        lead_value, through, opened = element
        carry_in = following * opened
        return (lead_value + through * carry_in, carry_in)

    _, carry_ins = lax.scan(
        back_step, jnp.zeros((H,), jnp.float32), (lead_seq.T, through_seq, open_next), reverse=True
    )
    own_carry = carry_ins[own_ids].T
    suffix = jnp.flip(jnp.cumsum(jnp.flip(cum_grad, axis=2), axis=2), axis=2)
    next_start = lax.cummin(jnp.where(own_starts, within[None, :], CH), axis=1, reverse=True)
    next_break = jnp.concatenate([next_start[:, 1:], jnp.full((2, 1), CH, jnp.int32)], axis=1)
    padded = jnp.concatenate([suffix, jnp.zeros((H, 2, 1), jnp.float32)], axis=2)
    beyond = jnp.take_along_axis(padded, jnp.broadcast_to(next_break[None], (H, 2, CH)), axis=2)
    grad_log = (
        suffix - beyond + (next_break == CH)[None].astype(jnp.float32) * own_carry[:, :, None]
    )
    grad_logit = (grad_log.reshape(H, tokens).T * jax.nn.sigmoid(-gate_logit)).astype(jnp.bfloat16)
    grad_proj = jnp.concatenate(
        [
            grad_q_acc.transpose(1, 0, 2).reshape(tokens, D).astype(jnp.bfloat16),
            grad_keys.astype(jnp.bfloat16),
            grad_values.astype(jnp.bfloat16),
        ],
        axis=1,
    )
    d_qkv = matmul_first(attn_in, grad_proj).reshape(D, 3, D).transpose(1, 0, 2)
    d_forget_w = matmul_first(attn_in, grad_logit)
    d_forget_b = jnp.sum(grad_logit.astype(jnp.float32), axis=0)
    grad_normed_one = matmul_last(grad_proj, w_qkv) + matmul_last(grad_logit, w_forget)
    d_gain_one = jnp.sum(grad_normed_one * normed_one, axis=0)
    grad_input = grad_middle + rms_back(grad_normed_one, gains[0], normed_one, factor_one)
    red_qkv, red_out, red_in, red_down = (
        lax.psum_scatter(d_qkv, ("wide", "narrow"), scatter_dimension=1, tiled=True),
        lax.psum_scatter(d_out, ("wide", "narrow"), scatter_dimension=0, tiled=True),
        lax.psum_scatter(d_gate_up, ("wide", "narrow"), scatter_dimension=2, tiled=True),
        lax.psum_scatter(d_down, ("wide", "narrow"), scatter_dimension=0, tiled=True),
    )
    grad_list = (red_qkv[0], red_qkv[1], red_qkv[2], red_out, red_in[0].T, red_in[1].T, red_down)
    mom_list = (qkv_mom[0], qkv_mom[1], qkv_mom[2], out_mom, in_mom[0].T, in_mom[1].T, down_mom)
    old_list = (qkv_w[0], qkv_w[1], qkv_w[2], out_w, ffn_in[0].T, ffn_in[1].T, ffn_out)
    grad_squares = jnp.stack([jnp.sum(gradient * gradient) for gradient in grad_list])
    cross_terms = jnp.stack(
        [jnp.sum(gradient * moment) for gradient, moment in zip(grad_list, mom_list)]
    )
    moment_squares = jnp.stack([jnp.sum(moment * moment) for moment in mom_list])
    local_stats = jnp.stack([grad_squares, cross_terms, moment_squares], axis=1)
    d_gains = jnp.stack([d_gain_one, d_gain_two])
    sum_gains, sum_forget_w, sum_forget_b, stat_sums = lax.psum(
        (d_gains, d_forget_w, d_forget_b, local_stats), ("wide", "narrow")
    )
    square_total = (
        jnp.sum(stat_sums[:, 0])
        + jnp.sum(sum_gains * sum_gains)
        + jnp.sum(sum_forget_w * sum_forget_w)
        + jnp.sum(sum_forget_b * sum_forget_b)
    )
    grad_norm = jnp.sqrt(square_total)
    clip_factor = jnp.minimum(1.0, CLIP_NORM / (grad_norm + 1e-06))
    new_moms = [
        MOMENTUM * moment + clip_factor * gradient for gradient, moment in zip(grad_list, mom_list)
    ]
    directions = [
        clip_factor * gradient + MOMENTUM * new_moment
        for gradient, new_moment in zip(grad_list, new_moms)
    ]
    lead_coef = (1.0 + MOMENTUM) * clip_factor
    update_squares = (
        lead_coef * lead_coef * stat_sums[:, 0]
        + 2.0 * lead_coef * MOMENTUM * MOMENTUM * stat_sums[:, 1]
        + MOMENTUM**4 * stat_sums[:, 2]
    )
    starting = [
        (direction / (jnp.sqrt(update_squares[number]) + 1e-07)).astype(jnp.bfloat16)
        for number, direction in enumerate(directions)
    ]
    current = (
        lax.all_gather(starting[0], "wide", axis=0, tiled=True),
        lax.all_gather(starting[1], "wide", axis=0, tiled=True),
        lax.all_gather(starting[2], "wide", axis=0, tiled=True),
        lax.all_gather(starting[3], "wide", axis=0, tiled=True),
        lax.all_gather(starting[4], "wide", axis=0, tiled=True),
        lax.all_gather(starting[5], "wide", axis=0, tiled=True),
        lax.all_gather(starting[6], "wide", axis=0, tiled=True),
    )
    for sweep_number in range(SWEEPS):
        columns = [column_block(row_block, wide_rank, wide_count) for row_block in current]
        parts = [matmul_first(row_block, column) for row_block, column in zip(current, columns)]
        grams = lax.psum(
            (parts[0], parts[1], parts[2], parts[3], parts[4], parts[5], parts[6]), "narrow"
        )
        products = [
            jnp.dot(
                row_block, gram_block.astype(jnp.bfloat16), preferred_element_type=jnp.float32
            ).astype(jnp.bfloat16)
            for row_block, gram_block in zip(current, grams)
        ]
        halves = [matmul_first(row_block, product) for row_block, product in zip(current, products)]
        squares = lax.psum(
            (halves[0], halves[1], halves[2], halves[3], halves[4], halves[5], halves[6]), "narrow"
        )
        updated = [
            (
                COEF_LINEAR * column.astype(jnp.float32)
                + jnp.dot(
                    row_block,
                    (COEF_CUBIC * gram_block + COEF_QUINTIC * square).astype(jnp.bfloat16),
                    preferred_element_type=jnp.float32,
                )
            ).astype(jnp.bfloat16)
            for row_block, column, gram_block, square in zip(current, columns, grams, squares)
        ]
        current = (
            lax.all_gather(updated[0], "wide", axis=1, tiled=True),
            lax.all_gather(updated[1], "wide", axis=1, tiled=True),
            lax.all_gather(updated[2], "wide", axis=1, tiled=True),
            lax.all_gather(updated[3], "wide", axis=1, tiled=True),
            lax.all_gather(updated[4], "wide", axis=1, tiled=True),
            lax.all_gather(updated[5], "wide", axis=1, tiled=True),
            lax.all_gather(updated[6], "wide", axis=1, tiled=True),
        )
    ortho_rows = [
        lax.dynamic_slice_in_dim(
            row_block,
            wide_rank * (row_block.shape[0] // wide_count),
            row_block.shape[0] // wide_count,
            0,
        ).astype(jnp.float32)
        for row_block in current
    ]
    rates = [
        tall_rate(D, D, D),
        tall_rate(D, D, D),
        tall_rate(D, D, D),
        tall_rate(D, D, D // 32),
        tall_rate(FF, D, D),
        tall_rate(FF, D, D),
        tall_rate(FF, D, FF),
    ]
    new_list = [
        (1.0 - MUON_DECAY) * previous - step_rate * ortho
        for previous, step_rate, ortho in zip(old_list, rates, ortho_rows)
    ]
    bias_one = 1.0 - BETA_FIRST**STEP
    bias_two = 1.0 - BETA_SECOND**STEP
    gains_new, gains_first, gains_second = adam_update(
        gains, gains_m, gains_v, clip_factor * sum_gains, bias_one, bias_two, RATE_GAINS
    )
    forget_w_new, forget_w_first, forget_w_second = adam_update(
        fgate_w, fgate_w_m, fgate_w_v, clip_factor * sum_forget_w, bias_one, bias_two, RATE_FGATE_W
    )
    forget_b_new, forget_b_first, forget_b_second = adam_update(
        fgate_b, fgate_b_m, fgate_b_v, clip_factor * sum_forget_b, bias_one, bias_two, RATE_FGATE_B
    )
    return (
        result.astype(jnp.bfloat16)[None],
        grad_input[None],
        grad_norm.reshape(1),
        jnp.stack(new_list[0:3]),
        new_list[3],
        jnp.stack([new_list[4].T, new_list[5].T]),
        new_list[6],
        jnp.stack(new_moms[0:3]),
        new_moms[3],
        jnp.stack([new_moms[4].T, new_moms[5].T]),
        new_moms[6],
        gains_new,
        gains_first,
        gains_second,
        forget_w_new,
        forget_w_first,
        forget_w_second,
        forget_b_new,
        forget_b_first,
        forget_b_second,
    )


def solution(mesh):
    placed = (
        P("narrow", "wide", None),
        P("narrow", "wide", None),
        P(None, ("wide", "narrow"), None),
        P(("wide", "narrow"), None),
        P(None, None, ("wide", "narrow")),
        P(("wide", "narrow"), None),
        P(None, ("wide", "narrow"), None),
        P(("wide", "narrow"), None),
        P(None, None, ("wide", "narrow")),
        P(("wide", "narrow"), None),
        P(),
        P(),
        P(),
        P(),
        P(),
        P(),
        P(),
        P(),
        P(),
        P("narrow", None),
        P("narrow", None),
        P("narrow", None, None),
    )
    return jax.shard_map(
        shards,
        mesh=mesh,
        in_specs=placed,
        out_specs=(
            P("narrow", "wide", None),
            P("narrow", "wide", None),
            P(),
            P(None, ("wide", "narrow"), None),
            P(("wide", "narrow"), None),
            P(None, None, ("wide", "narrow")),
            P(("wide", "narrow"), None),
            P(None, ("wide", "narrow"), None),
            P(("wide", "narrow"), None),
            P(None, None, ("wide", "narrow")),
            P(("wide", "narrow"), None),
            P(),
            P(),
            P(),
            P(),
            P(),
            P(),
            P(),
            P(),
            P(),
        ),
        check_vma=False,
    )
```

profile of v0, /device:TPU:0, one launch (start us, length us, event | category | flops | bytes accessed | tf_op | source)
XLA Modules:
  0.0 6341.4 jit_solution(16646949531855203917)
XLA Ops:
  9.6 107.9 %all-gather.52.cloned.1.call-done = bf16[3,1536,1536]{2,1,0:T(8,128)(2,1)} async-done(((bf16[3,48,1536]{2,1,0:T(8,128)(2,1)}), bf16[3,1536,1536]{2,1,0:T(8,128)(2,1)}) %all-gather.52.cloned.1.call-update) | async-done | bytes 14155792 | tf_op jit(solution)/shard_map/all_gather | solution.py:124
  169.7 25.0 gather_fusion.11
  194.7 30.7 all_gather.163
  268.1 156.0 %while.70 = (s32[]{:T(128)}, f32[24,128]{1,0:T(8,128)S(1)}, f32[24,128]{1,0:T(8,128)S(1)}, f32[24,128,64]{1,2,0:T(8,128)S(1)}, s32[16]{0:T(128)S(1)}, /*index=5*...) while((s32[]{:T(128)}, f32[24,128]{1,0:T(8,128)S(1)}, ...), condition=%wide.region_13.15_spmd, body=%wide.region_7.14_spmd.sunk | while | flops 52968968 | bytes 6204007 | solution.py:66
  428.8 61.9 all-gather.60.cloned.1.call-done
  505.8 82.4 %all-gather.62.cloned.1.call-done = bf16[4096,1536]{1,0:T(8,128)(2,1)} async-done(((bf16[128,1536]{1,0:T(8,128)(2,1)}), bf16[4096,1536]{1,0:T(8,128)(2,1)}) %all-gather.62.cloned.1.call-update) | async-done | bytes 12582928 | tf_op jit(solution)/shard_map/all_gather | solution.py:127
  616.1 205.8 %while.71 = (s32[]{:T(128)}, f32[24,128,64]{1,2,0:T(8,128)S(1)}, f32[24,128]{1,0:T(8,128)}, s32[16]{0:T(128)}, s32[1024]{0:T(1024)}, /*index=5*/s32[128]{0:T(128...) while((s32[]{:T(128)}, f32[24,128,64]{1,2,0:T(8,128)S(1)}, ...), condition=%wide.region_22.24_spmd, body=%wide.region_17.23_spmd.sunk | while | flops 77932040 | bytes 7049899 | solution.py:66
  822.8 48.5 all_gather.169
  876.9 162.6 %while.72 = (s32[]{:T(128)}, f32[128,24,64]{0,2,1:T(8,128)S(1)}, f32[128,24,64]{0,2,1:T(8,128)S(1)}, f32[24,128]{1,0:T(8,128)S(1)}, s32[128]{0:T(128)}, /*index=...) while((s32[]{:T(128)}, f32[128,24,64]{0,2,1:T(8,128)S(1)}, ...), condition=%wide.region_28.30_spmd, body=%wide.region_23.29_spmd.sunk | while | flops 103484744 | bytes 9631449 | solution.py:66
  1041.3 24.1 gather_fusion.12
  1084.6 40.5 while.74
  1138.6 37.5 copy.686
  1212.4 49.5 copy.691
  1281.8 453.4 %all-reduce.27.cloned.1.call-done = (f32[3,1536,1536]{2,0,1:T(4,128)}, f32[1536,24]{0,1:T(8,128)}) async-done(((f32[3,1536,1536]{2,0,1:T(4,128)}, f32[1536,24]{0,1:T(8,128)}), (f32[3,1536,1536]{2,0,1:T(4,128)}, f32[1536,24]{0,1:T(8,128)})) %all-reduce.27.cloned.1.call-update) | async-done | bytes 28459024
  1742.4 242.1 %reduce-scatter.8.cloned.1.call-done = f32[128,1536]{0,1:T(8,128)} async-done(((f32[4096,1536]{0,1:T(8,128)}), f32[128,1536]{0,1:T(8,128)}) %reduce-scatter.8.cloned.1.call-update) | async-done | bytes 786448 | tf_op jit(solution)/shard_map/reduce_scatter | solution.py:422
  1986.6 435.5 %reduce-scatter.6.cloned.1.call-done = f32[2,1536,128]{2,1,0:T(8,128)} async-done(((f32[2,1536,4096]{2,1,0:T(8,128)}), f32[2,1536,128]{2,1,0:T(8,128)}) %reduce-scatter.6.cloned.1.call-update) | async-done | bytes 1572880 | tf_op jit(solution)/shard_map/reduce_scatter | solution.py:421
  2438.1 39.3 all-reduce.3
  2500.1 27.5 all-gather.92.cloned.1.call-done
  2528.9 41.5 all-gather.80.cloned.1.call-done
  2571.5 41.6 all-gather.68.cloned.1.call-done
  2614.8 40.9 all-gather.104.cloned.1.call-done
  2663.0 56.7 all-gather.128.cloned.1.call-done
  2723.9 59.7 all-gather.116.cloned.1.call-done
  2787.8 59.9 all-gather.140.cloned.1.call-done
  2852.0 151.5 %all-reduce.47.cloned.1.call-done = (f32[1536,192]{0,1:T(8,128)}, f32[1536,192]{0,1:T(8,128)}, f32[1536,192]{0,1:T(8,128)}, f32[1536,192]{0,1:T(8,128)}, f32[153...) async-done(((f32[1536,192]{0,1:T(8,128)}, f32[1536,192]{0,1:T(8,128)}, f32[1536,192]{0,1:T(8,128)}, f32[1536,192]{0,1:T(8,128)}, f32[1536,192]{0,1:T(8,128)}, ...) | async-done | bytes 8257552 | tf_op jit(solution)/shard_map/psum | solution.py:474
  3033.9 152.2 %all-reduce.45.cloned.1.call-done = (f32[1536,192]{0,1:T(8,128)}, f32[1536,192]{0,1:T(8,128)}, f32[1536,192]{0,1:T(8,128)}, f32[1536,192]{0,1:T(8,128)}, f32[153...) async-done(((f32[1536,192]{0,1:T(8,128)}, f32[1536,192]{0,1:T(8,128)}, f32[1536,192]{0,1:T(8,128)}, f32[1536,192]{0,1:T(8,128)}, f32[1536,192]{0,1:T(8,128)}, ...) | async-done | bytes 8257552 | tf_op jit(solution)/shard_map/psum | solution.py:484
  3233.6 40.0 all-gather.82.cloned.1.call-done
  3276.4 39.8 all-gather.70.cloned.1.call-done
  3319.2 40.0 all-gather.106.cloned.1.call-done
  3362.0 59.2 all-gather.130.cloned.1.call-done
  3425.4 57.7 all-gather.118.cloned.1.call-done
  3487.3 57.4 all-gather.142.cloned.1.call-done
  3549.1 151.9 %all-reduce.43.cloned.1.call-done = (f32[1536,192]{0,1:T(8,128)}, f32[1536,192]{0,1:T(8,128)}, f32[1536,192]{0,1:T(8,128)}, f32[1536,192]{0,1:T(8,128)}, f32[153...) async-done(((f32[1536,192]{0,1:T(8,128)}, f32[1536,192]{0,1:T(8,128)}, f32[1536,192]{0,1:T(8,128)}, f32[1536,192]{0,1:T(8,128)}, f32[1536,192]{0,1:T(8,128)}, ...) | async-done | bytes 8257552 | tf_op jit(solution)/shard_map/psum | solution.py:474
  3730.1 153.2 %all-reduce.41.cloned.1.call-done = (f32[1536,192]{0,1:T(8,128)}, f32[1536,192]{0,1:T(8,128)}, f32[1536,192]{0,1:T(8,128)}, f32[1536,192]{0,1:T(8,128)}, f32[153...) async-done(((f32[1536,192]{0,1:T(8,128)}, f32[1536,192]{0,1:T(8,128)}, f32[1536,192]{0,1:T(8,128)}, f32[1536,192]{0,1:T(8,128)}, f32[1536,192]{0,1:T(8,128)}, ...) | async-done | bytes 8257552 | tf_op jit(solution)/shard_map/psum | solution.py:484
  3930.6 40.0 all-gather.84.cloned.1.call-done
  3973.5 39.8 all-gather.72.cloned.1.call-done
  4016.2 40.0 all-gather.108.cloned.1.call-done
  4059.0 59.4 all-gather.132.cloned.1.call-done
  4122.6 57.7 all-gather.120.cloned.1.call-done
  4184.5 57.2 all-gather.144.cloned.1.call-done
  4246.0 152.1 %all-reduce.39.cloned.1.call-done = (f32[1536,192]{0,1:T(8,128)}, f32[1536,192]{0,1:T(8,128)}, f32[1536,192]{0,1:T(8,128)}, f32[1536,192]{0,1:T(8,128)}, f32[153...) async-done(((f32[1536,192]{0,1:T(8,128)}, f32[1536,192]{0,1:T(8,128)}, f32[1536,192]{0,1:T(8,128)}, f32[1536,192]{0,1:T(8,128)}, f32[1536,192]{0,1:T(8,128)}, ...) | async-done | bytes 8257552 | tf_op jit(solution)/shard_map/psum | solution.py:474
  4427.1 153.2 %all-reduce.37.cloned.1.call-done = (f32[1536,192]{0,1:T(8,128)}, f32[1536,192]{0,1:T(8,128)}, f32[1536,192]{0,1:T(8,128)}, f32[1536,192]{0,1:T(8,128)}, f32[153...) async-done(((f32[1536,192]{0,1:T(8,128)}, f32[1536,192]{0,1:T(8,128)}, f32[1536,192]{0,1:T(8,128)}, f32[1536,192]{0,1:T(8,128)}, f32[1536,192]{0,1:T(8,128)}, ...) | async-done | bytes 8257552 | tf_op jit(solution)/shard_map/psum | solution.py:484
  4627.7 40.0 all-gather.86.cloned.1.call-done
  4670.5 40.0 all-gather.74.cloned.1.call-done
  4713.5 39.7 all-gather.110.cloned.1.call-done
  4756.1 59.4 all-gather.134.cloned.1.call-done
  4819.7 57.8 all-gather.122.cloned.1.call-done
  4881.6 57.2 all-gather.146.cloned.1.call-done
  4943.2 151.7 %all-reduce.35.cloned.1.call-done = (f32[1536,192]{0,1:T(8,128)}, f32[1536,192]{0,1:T(8,128)}, f32[1536,192]{0,1:T(8,128)}, f32[1536,192]{0,1:T(8,128)}, f32[153...) async-done(((f32[1536,192]{0,1:T(8,128)}, f32[1536,192]{0,1:T(8,128)}, f32[1536,192]{0,1:T(8,128)}, f32[1536,192]{0,1:T(8,128)}, f32[1536,192]{0,1:T(8,128)}, ...) | async-done | bytes 8257552 | tf_op jit(solution)/shard_map/psum | solution.py:474
  5124.2 153.2 %all-reduce.33.cloned.1.call-done = (f32[1536,192]{0,1:T(8,128)}, f32[1536,192]{0,1:T(8,128)}, f32[1536,192]{0,1:T(8,128)}, f32[1536,192]{0,1:T(8,128)}, f32[153...) async-done(((f32[1536,192]{0,1:T(8,128)}, f32[1536,192]{0,1:T(8,128)}, f32[1536,192]{0,1:T(8,128)}, f32[1536,192]{0,1:T(8,128)}, f32[1536,192]{0,1:T(8,128)}, ...) | async-done | bytes 8257552 | tf_op jit(solution)/shard_map/psum | solution.py:484
  5324.7 40.0 all-gather.88.cloned.1.call-done
  5367.6 39.8 all-gather.76.cloned.1.call-done
  5410.3 40.0 all-gather.112.cloned.1.call-done
  5453.1 59.2 all-gather.136.cloned.1.call-done
  5516.5 58.0 all-gather.124.cloned.1.call-done
  5578.7 57.3 all-gather.148.cloned.1.call-done
  5640.2 152.1 %all-reduce.31.cloned.1.call-done = (f32[1536,192]{0,1:T(8,128)}, f32[1536,192]{0,1:T(8,128)}, f32[1536,192]{0,1:T(8,128)}, f32[1536,192]{0,1:T(8,128)}, f32[153...) async-done(((f32[1536,192]{0,1:T(8,128)}, f32[1536,192]{0,1:T(8,128)}, f32[1536,192]{0,1:T(8,128)}, f32[1536,192]{0,1:T(8,128)}, f32[1536,192]{0,1:T(8,128)}, ...) | async-done | bytes 8257552 | tf_op jit(solution)/shard_map/psum | solution.py:474
  5821.5 153.2 %all-reduce.29.cloned.1.call-done = (f32[1536,192]{0,1:T(8,128)}, f32[1536,192]{0,1:T(8,128)}, f32[1536,192]{0,1:T(8,128)}, f32[1536,192]{0,1:T(8,128)}, f32[153...) async-done(((f32[1536,192]{0,1:T(8,128)}, f32[1536,192]{0,1:T(8,128)}, f32[1536,192]{0,1:T(8,128)}, f32[1536,192]{0,1:T(8,128)}, f32[1536,192]{0,1:T(8,128)}, ...) | async-done | bytes 8257552 | tf_op jit(solution)/shard_map/psum | solution.py:484
  6028.2 33.2 all-gather.90.cloned.1.call-done
  6063.0 40.7 all-gather.78.cloned.1.call-done
  6105.2 40.7 all-gather.114.cloned.1.call-done
  6149.2 58.4 all-gather.150.cloned.1.call-done
  6209.9 59.1 all-gather.126.cloned.1.call-done
  6269.0 61.4 all-gather.138.cloned.1.call-done
  (1754 shorter events, 1449.5 us)
Async XLA Ops:
  7.2 110.3 %all-gather.52.cloned.1.call-start = ((), (), s32[]{:S(2)}) async-start(), calls=%async_computation.3 | async-start | bytes 14598144 | tf_op jit(solution)/shard_map/all_gather | solution.py:124
  9.3 246.7 %all-gather.56.cloned.1.call-start = ((), (), s32[]{:S(2)}) async-start(), calls=%async_computation.5 | async-start | bytes 3538944 | tf_op jit(solution)/shard_map/all_gather | solution.py:239
  146.8 121.2 %all-gather.54.cloned.1.call-start = ((), (), s32[]{:S(2)}) async-start(), calls=%async_computation.4 | async-start | bytes 3538944 | tf_op jit(solution)/shard_map/all_gather | solution.py:238
  147.5 276.8 %all-gather.58.cloned.1.call-start = ((), (), s32[]{:S(2)}) async-start(), calls=%async_computation.6 | async-start | bytes 4866048 | tf_op jit(solution)/shard_map/all_gather | solution.py:125
  148.3 342.4 %all-gather.60.cloned.1.call-start = ((), (), s32[]{:S(2)}) async-start(), calls=%async_computation.7 | async-start | bytes 25952256 | tf_op jit(solution)/shard_map/all_gather | solution.py:126
  149.6 438.6 %all-gather.62.cloned.1.call-start = ((), (), s32[]{:S(2)}) async-start(), calls=%async_computation.8 | async-start | bytes 12976128 | tf_op jit(solution)/shard_map/all_gather | solution.py:127
  150.4 725.9 %all-gather.64.cloned.1.call-start = ((), (), s32[]{:S(2)}) async-start(), calls=%async_computation.9 | async-start | bytes 3538944 | tf_op jit(solution)/shard_map/all_gather | solution.py:365
  255.8 620.5 %all-gather.66.cloned.1.call-start = ((), (), s32[]{:S(2)}) async-start(), calls=%async_computation.10 | async-start | bytes 3538944 | tf_op jit(solution)/shard_map/all_gather | solution.py:366
  614.6 665.1 %reduce-scatter.10.cloned.1.call-start = ((), (), s32[]{:S(2)}) async-start(), calls=%async_computation.55 | async-start | bytes 9732096 | tf_op jit(solution)/shard_map/reduce_scatter | solution.py:420
  876.2 859.0 %all-reduce.27.cloned.1.call-start = ((), (), s32[]{:S(2)}) async-start(), calls=%async_computation.56 | async-start | bytes 75792384
  1177.6 806.9 %reduce-scatter.8.cloned.1.call-start = ((), (), s32[]{:S(2)}) async-start(), calls=%async_computation.12 | async-start | bytes 25952256 | tf_op jit(solution)/shard_map/reduce_scatter | solution.py:422
  1190.2 1231.9 %reduce-scatter.6.cloned.1.call-start = ((), (), s32[]{:S(2)}) async-start(), calls=%async_computation.11 | async-start | bytes 51904512 | tf_op jit(solution)/shard_map/reduce_scatter | solution.py:421
  1261.9 1265.8 %all-gather.92.cloned.1.call-start = ((), (), s32[]{:S(2)}) async-start(), calls=%async_computation.25 | async-start | bytes 1327104 | tf_op jit(solution)/shard_map/all_gather | solution.py:465
  2486.7 83.7 %all-gather.80.cloned.1.call-start = ((), (), s32[]{:S(2)}) async-start(), calls=%async_computation.19 | async-start | bytes 1327104 | tf_op jit(solution)/shard_map/all_gather | solution.py:464
  2490.3 122.8 %all-gather.68.cloned.1.call-start = ((), (), s32[]{:S(2)}) async-start(), calls=%async_computation.13 | async-start | bytes 1327104 | tf_op jit(solution)/shard_map/all_gather | solution.py:463
  2490.9 164.9 %all-gather.104.cloned.1.call-start = ((), (), s32[]{:S(2)}) async-start(), calls=%async_computation.31 | async-start | bytes 1327104 | tf_op jit(solution)/shard_map/all_gather | solution.py:466
  2493.5 226.2 %all-gather.128.cloned.1.call-start = ((), (), s32[]{:S(2)}) async-start(), calls=%async_computation.43 | async-start | bytes 3538944 | tf_op jit(solution)/shard_map/all_gather | solution.py:468
  2496.2 287.5 %all-gather.116.cloned.1.call-start = ((), (), s32[]{:S(2)}) async-start(), calls=%async_computation.37 | async-start | bytes 3538944 | tf_op jit(solution)/shard_map/all_gather | solution.py:467
  2496.8 351.0 %all-gather.140.cloned.1.call-start = ((), (), s32[]{:S(2)}) async-start(), calls=%async_computation.49 | async-start | bytes 3538944 | tf_op jit(solution)/shard_map/all_gather | solution.py:469
  2499.9 503.6 %all-reduce.47.cloned.1.call-start = ((), (), s32[]{:S(2)}) async-start(), calls=%async_computation.66 | async-start | bytes 16515072 | tf_op jit(solution)/shard_map/psum | solution.py:474
  2851.9 334.1 %all-reduce.45.cloned.1.call-start = ((), (), s32[]{:S(2)}) async-start(), calls=%async_computation.65 | async-start | bytes 16515072 | tf_op jit(solution)/shard_map/psum | solution.py:484
  3032.8 197.9 %all-gather.94.cloned.1.call-start = ((), (), s32[]{:S(2)}) async-start(), calls=%async_computation.26 | async-start | bytes 1327104 | tf_op jit(solution)/shard_map/all_gather | solution.py:501
  3189.3 84.2 %all-gather.82.cloned.1.call-start = ((), (), s32[]{:S(2)}) async-start(), calls=%async_computation.20 | async-start | bytes 1327104 | tf_op jit(solution)/shard_map/all_gather | solution.py:500
  3193.2 123.0 %all-gather.70.cloned.1.call-start = ((), (), s32[]{:S(2)}) async-start(), calls=%async_computation.14 | async-start | bytes 1327104 | tf_op jit(solution)/shard_map/all_gather | solution.py:499
  3196.8 162.4 %all-gather.106.cloned.1.call-start = ((), (), s32[]{:S(2)}) async-start(), calls=%async_computation.32 | async-start | bytes 1327104 | tf_op jit(solution)/shard_map/all_gather | solution.py:502
  3200.3 221.0 %all-gather.130.cloned.1.call-start = ((), (), s32[]{:S(2)}) async-start(), calls=%async_computation.44 | async-start | bytes 3538944 | tf_op jit(solution)/shard_map/all_gather | solution.py:504
  3204.6 278.5 %all-gather.118.cloned.1.call-start = ((), (), s32[]{:S(2)}) async-start(), calls=%async_computation.38 | async-start | bytes 3538944 | tf_op jit(solution)/shard_map/all_gather | solution.py:503
  3207.9 336.8 %all-gather.142.cloned.1.call-start = ((), (), s32[]{:S(2)}) async-start(), calls=%async_computation.50 | async-start | bytes 3538944 | tf_op jit(solution)/shard_map/all_gather | solution.py:505
  3212.2 488.8 %all-reduce.43.cloned.1.call-start = ((), (), s32[]{:S(2)}) async-start(), calls=%async_computation.64 | async-start | bytes 16515072 | tf_op jit(solution)/shard_map/psum | solution.py:474
  3548.9 334.4 %all-reduce.41.cloned.1.call-start = ((), (), s32[]{:S(2)}) async-start(), calls=%async_computation.63 | async-start | bytes 16515072 | tf_op jit(solution)/shard_map/psum | solution.py:484
  3730.0 197.7 %all-gather.96.cloned.1.call-start = ((), (), s32[]{:S(2)}) async-start(), calls=%async_computation.27 | async-start | bytes 1327104 | tf_op jit(solution)/shard_map/all_gather | solution.py:501
  3886.4 84.2 %all-gather.84.cloned.1.call-start = ((), (), s32[]{:S(2)}) async-start(), calls=%async_computation.21 | async-start | bytes 1327104 | tf_op jit(solution)/shard_map/all_gather | solution.py:500
  3889.6 123.7 %all-gather.72.cloned.1.call-start = ((), (), s32[]{:S(2)}) async-start(), calls=%async_computation.15 | async-start | bytes 1327104 | tf_op jit(solution)/shard_map/all_gather | solution.py:499
  3892.9 163.3 %all-gather.108.cloned.1.call-start = ((), (), s32[]{:S(2)}) async-start(), calls=%async_computation.33 | async-start | bytes 1327104 | tf_op jit(solution)/shard_map/all_gather | solution.py:502
  3896.1 222.3 %all-gather.132.cloned.1.call-start = ((), (), s32[]{:S(2)}) async-start(), calls=%async_computation.45 | async-start | bytes 3538944 | tf_op jit(solution)/shard_map/all_gather | solution.py:504
  3899.4 280.9 %all-gather.120.cloned.1.call-start = ((), (), s32[]{:S(2)}) async-start(), calls=%async_computation.39 | async-start | bytes 3538944 | tf_op jit(solution)/shard_map/all_gather | solution.py:503
  3903.8 337.9 %all-gather.144.cloned.1.call-start = ((), (), s32[]{:S(2)}) async-start(), calls=%async_computation.51 | async-start | bytes 3538944 | tf_op jit(solution)/shard_map/all_gather | solution.py:505
  3907.1 490.9 %all-reduce.39.cloned.1.call-start = ((), (), s32[]{:S(2)}) async-start(), calls=%async_computation.62 | async-start | bytes 16515072 | tf_op jit(solution)/shard_map/psum | solution.py:474
  4245.9 334.4 %all-reduce.37.cloned.1.call-start = ((), (), s32[]{:S(2)}) async-start(), calls=%async_computation.61 | async-start | bytes 16515072 | tf_op jit(solution)/shard_map/psum | solution.py:484
  4427.1 197.7 %all-gather.98.cloned.1.call-start = ((), (), s32[]{:S(2)}) async-start(), calls=%async_computation.28 | async-start | bytes 1327104 | tf_op jit(solution)/shard_map/all_gather | solution.py:501
  4583.5 84.2 %all-gather.86.cloned.1.call-start = ((), (), s32[]{:S(2)}) async-start(), calls=%async_computation.22 | async-start | bytes 1327104 | tf_op jit(solution)/shard_map/all_gather | solution.py:500
  4586.7 123.9 %all-gather.74.cloned.1.call-start = ((), (), s32[]{:S(2)}) async-start(), calls=%async_computation.16 | async-start | bytes 1327104 | tf_op jit(solution)/shard_map/all_gather | solution.py:499
  4590.3 163.0 %all-gather.110.cloned.1.call-start = ((), (), s32[]{:S(2)}) async-start(), calls=%async_computation.34 | async-start | bytes 1327104 | tf_op jit(solution)/shard_map/all_gather | solution.py:502
  4593.6 221.9 %all-gather.134.cloned.1.call-start = ((), (), s32[]{:S(2)}) async-start(), calls=%async_computation.46 | async-start | bytes 3538944 | tf_op jit(solution)/shard_map/all_gather | solution.py:504
  4596.8 280.6 %all-gather.122.cloned.1.call-start = ((), (), s32[]{:S(2)}) async-start(), calls=%async_computation.40 | async-start | bytes 3538944 | tf_op jit(solution)/shard_map/all_gather | solution.py:503
  4601.2 337.6 %all-gather.146.cloned.1.call-start = ((), (), s32[]{:S(2)}) async-start(), calls=%async_computation.52 | async-start | bytes 3538944 | tf_op jit(solution)/shard_map/all_gather | solution.py:505
  4604.5 490.4 %all-reduce.35.cloned.1.call-start = ((), (), s32[]{:S(2)}) async-start(), calls=%async_computation.60 | async-start | bytes 16515072 | tf_op jit(solution)/shard_map/psum | solution.py:474
  4943.0 334.4 %all-reduce.33.cloned.1.call-start = ((), (), s32[]{:S(2)}) async-start(), calls=%async_computation.59 | async-start | bytes 16515072 | tf_op jit(solution)/shard_map/psum | solution.py:484
  5124.2 197.7 %all-gather.100.cloned.1.call-start = ((), (), s32[]{:S(2)}) async-start(), calls=%async_computation.29 | async-start | bytes 1327104 | tf_op jit(solution)/shard_map/all_gather | solution.py:501
  5280.5 84.2 %all-gather.88.cloned.1.call-start = ((), (), s32[]{:S(2)}) async-start(), calls=%async_computation.23 | async-start | bytes 1327104 | tf_op jit(solution)/shard_map/all_gather | solution.py:500
  5283.7 123.7 %all-gather.76.cloned.1.call-start = ((), (), s32[]{:S(2)}) async-start(), calls=%async_computation.17 | async-start | bytes 1327104 | tf_op jit(solution)/shard_map/all_gather | solution.py:499
  5287.0 163.3 %all-gather.112.cloned.1.call-start = ((), (), s32[]{:S(2)}) async-start(), calls=%async_computation.35 | async-start | bytes 1327104 | tf_op jit(solution)/shard_map/all_gather | solution.py:502
  5290.2 222.1 %all-gather.136.cloned.1.call-start = ((), (), s32[]{:S(2)}) async-start(), calls=%async_computation.47 | async-start | bytes 3538944 | tf_op jit(solution)/shard_map/all_gather | solution.py:504
  5293.5 281.0 %all-gather.124.cloned.1.call-start = ((), (), s32[]{:S(2)}) async-start(), calls=%async_computation.41 | async-start | bytes 3538944 | tf_op jit(solution)/shard_map/all_gather | solution.py:503
  5297.9 338.1 %all-gather.148.cloned.1.call-start = ((), (), s32[]{:S(2)}) async-start(), calls=%async_computation.53 | async-start | bytes 3538944 | tf_op jit(solution)/shard_map/all_gather | solution.py:505
  5301.2 491.1 %all-reduce.31.cloned.1.call-start = ((), (), s32[]{:S(2)}) async-start(), calls=%async_computation.58 | async-start | bytes 16515072 | tf_op jit(solution)/shard_map/psum | solution.py:474
  5640.2 334.5 %all-reduce.29.cloned.1.call-start = ((), (), s32[]{:S(2)}) async-start(), calls=%async_computation.57 | async-start | bytes 16515072 | tf_op jit(solution)/shard_map/psum | solution.py:484
  5821.5 205.0 %all-gather.102.cloned.1.call-start = ((), (), s32[]{:S(2)}) async-start(), calls=%async_computation.30 | async-start | bytes 1327104 | tf_op jit(solution)/shard_map/all_gather | solution.py:501
  5977.8 83.5 %all-gather.90.cloned.1.call-start = ((), (), s32[]{:S(2)}) async-start(), calls=%async_computation.24 | async-start | bytes 1327104 | tf_op jit(solution)/shard_map/all_gather | solution.py:500
  5981.1 122.6 %all-gather.78.cloned.1.call-start = ((), (), s32[]{:S(2)}) async-start(), calls=%async_computation.18 | async-start | bytes 1327104 | tf_op jit(solution)/shard_map/all_gather | solution.py:499
  5984.5 161.4 %all-gather.114.cloned.1.call-start = ((), (), s32[]{:S(2)}) async-start(), calls=%async_computation.36 | async-start | bytes 1327104 | tf_op jit(solution)/shard_map/all_gather | solution.py:502
  5987.8 219.8 %all-gather.150.cloned.1.call-start = ((), (), s32[]{:S(2)}) async-start(), calls=%async_computation.54 | async-start | bytes 3538944 | tf_op jit(solution)/shard_map/all_gather | solution.py:505
  5992.1 276.9 %all-gather.126.cloned.1.call-start = ((), (), s32[]{:S(2)}) async-start(), calls=%async_computation.42 | async-start | bytes 3538944 | tf_op jit(solution)/shard_map/all_gather | solution.py:503
  5996.4 333.9 %all-gather.138.cloned.1.call-start = ((), (), s32[]{:S(2)}) async-start(), calls=%async_computation.48 | async-start | bytes 3538944 | tf_op jit(solution)/shard_map/all_gather | solution.py:504
  (165 other events, 7484.5 us)
Sparse Core Ops, SparseCore 0:
  11.6 105.9 all-gather.51
  146.9 58.9 all-gather.55
  208.7 59.2 all-gather.53
  271.3 62.7 all-gather.57
  337.3 153.3 all-gather.59
  494.0 94.1 all-gather.61
  590.9 58.7 all-gather.63
  652.4 59.1 all-gather.65
  876.3 145.5 reduce-scatter.9
  1177.8 557.4 all-reduce.26
  1741.7 242.8 reduce-scatter.7
  1992.0 430.0 reduce-scatter.5
  2486.8 40.8 all-gather.91
  2530.5 39.8 all-gather.79
  2573.2 39.8 all-gather.67
  2615.9 39.8 all-gather.103
  2657.9 61.8 all-gather.127
  2722.4 61.2 all-gather.115
  2786.5 61.2 all-gather.139
  2852.3 151.0 all-reduce.46
  3032.9 153.0 all-reduce.44
  3189.5 41.2 all-gather.93
  3233.7 39.8 all-gather.81
  3276.4 39.8 all-gather.69
  3319.3 39.8 all-gather.105
  3362.0 59.2 all-gather.129
  3424.0 59.0 all-gather.117
  3485.6 59.0 all-gather.141
  3549.4 151.5 all-reduce.42
  3730.1 153.0 all-reduce.40
  3886.5 41.2 all-gather.95
  3930.8 39.8 all-gather.83
  3973.4 39.8 all-gather.71
  4016.3 39.8 all-gather.107
  4059.1 59.2 all-gather.131
  4121.2 59.0 all-gather.119
  4182.6 59.0 all-gather.143
  4246.5 151.5 all-reduce.38
  4427.2 153.0 all-reduce.36
  4583.6 41.2 all-gather.97
  4627.8 39.8 all-gather.85
  4670.7 39.8 all-gather.73
  4713.4 39.8 all-gather.109
  4756.2 59.2 all-gather.133
  4818.3 59.0 all-gather.121
  4879.7 59.0 all-gather.145
  4943.4 151.5 all-reduce.34
  5124.3 153.0 all-reduce.32
  5280.6 41.2 all-gather.99
  5324.9 39.8 all-gather.87
  5367.6 39.8 all-gather.75
  5410.4 39.8 all-gather.111
  5453.1 59.2 all-gather.135
  5515.4 59.0 all-gather.123
  5576.9 59.0 all-gather.147
  5640.7 151.5 all-reduce.30
  5821.6 153.0 all-reduce.28
  5978.0 41.2 all-gather.101
  6021.5 39.8 all-gather.89
  6063.8 39.8 all-gather.77
  6106.1 39.8 all-gather.113
  6148.3 59.2 all-gather.149
  6209.9 59.0 all-gather.125
  6271.2 59.0 all-gather.137
where the time goes:
time: 6360 us; the launch traced here: 6340 us
  waiting for transfers between devices  4790 us (75%)
  local copies, waits for them, and re-layouts  564 us (9%)
  matrix products  551 us (9%)
  other arithmetic  199 us (3%)
  blocking collectives  137 us (2%)
  loops' own time  66.8 us (1%)
    psum x5, waiting for transfers between devices, shards(): lax.psum((halves[0], halves[1], halves[2], halves[3], halves[4], halves[5...  765 us
    psum x5, waiting for transfers between devices, shards(): lax.psum((parts[0], parts[1], parts[2], parts[3], parts[4], parts[5], par...  759 us
    unnamed x65, waiting for transfers between devices  456 us
    reduce_scatter x1, waiting for transfers between devices, shards(): lax.psum_scatter(d_gate_up, ('wide', 'narrow'), scatter_dimension=2, tile...  436 us
    dot_general x74, matrix products, matmul_first(): lax.dot_general(left, right, (((0,), (0,)), ((), ())), preferred_element_...  304 us
    all_gather x5, waiting for transfers between devices, shards(): lax.all_gather(updated[5], 'wide', axis=1, tiled=True)  299 us
    all_gather x5, waiting for transfers between devices, shards(): lax.all_gather(updated[4], 'wide', axis=1, tiled=True)  290 us
    all_gather x5, waiting for transfers between devices, shards(): lax.all_gather(updated[6], 'wide', axis=1, tiled=True)  288 us
  transfers between devices with their start and end apart: 64, of which 58 were waited for; matrix products, arithmetic and copies ran while one was open for 17% of the time, Pallas kernels for 0%

commit v1 on v0

v1 whole, which is shorter than its diff:
```python
import math

import jax
import jax.numpy as jnp
from jax import lax
from jax.sharding import PartitionSpec as P

D = 1536
H = 24
DH = 64
FF = 4096
SWEEPS = 5
STEP = 10
CH = 64


NORM_EPSILON = 1e-06
MASKED_SCORE = -1e30
COEF_LINEAR = 3.4445
COEF_CUBIC = -4.775
COEF_QUINTIC = 2.0315
MOMENTUM = 0.95
MUON_DECAY = 0.01
MUON_RATE = 0.5
BETA_FIRST = 0.9
BETA_SECOND = 0.95
ADAM_EPSILON = 1e-08
ADAM_DECAY = 0.1
RATE_GAINS = 1.0
RATE_FGATE_W = 0.03
RATE_FGATE_B = 4.0
CLIP_NORM = 1.0


def rms_parts(hidden):
    factor = lax.rsqrt(jnp.mean(hidden * hidden, axis=-1, keepdims=True) + NORM_EPSILON)
    return (hidden * factor, factor)


def rms_back(grad_normed, gain, normed, factor):
    scaled = grad_normed * gain
    return factor * (scaled - normed * jnp.mean(scaled * normed, axis=-1, keepdims=True))


def matmul_first(left, right):
    return lax.dot_general(
        left, right, (((0,), (0,)), ((), ())), preferred_element_type=jnp.float32
    )


def matmul_last(left, right):
    return lax.dot_general(
        left, right, (((1,), (1,)), ((), ())), preferred_element_type=jnp.float32
    )


def adam_update(weight, first, second, gradient, bias_one, bias_two, step_rate):
    new_first = BETA_FIRST * first + (1.0 - BETA_FIRST) * gradient
    new_second = BETA_SECOND * second + (1.0 - BETA_SECOND) * gradient * gradient
    update = new_first / bias_one / (jnp.sqrt(new_second / bias_two) + ADAM_EPSILON)
    return (weight - step_rate * (update + ADAM_DECAY * weight), new_first, new_second)


def tall_rate(rows_count, cols_count, fan_in):
    return MUON_RATE * math.sqrt(max(rows_count, cols_count) / fan_in)


def open_sum(mask, values):
    high = lax.reduce_precision(values, 8, 7)
    rest = values - high
    mid = lax.reduce_precision(rest, 8, 7)
    low = rest - mid
    count = values.shape[1]
    terms = jnp.concatenate([high, mid, low], axis=1).astype(jnp.bfloat16)
    sums = jnp.dot(mask, terms, preferred_element_type=jnp.float32)
    return sums[:, :count] + sums[:, count : 2 * count] + sums[:, 2 * count :]


def to_groups(chunks, first, rank, count):
    total = chunks.shape[0]
    received = []
    for shift in range(count):
        pick = jnp.clip((rank + shift) % count - first, 0, total - 1)
        chunk = lax.dynamic_index_in_dim(chunks, pick, 0, keepdims=False)
        if shift:
            pairs = [
                (place, (place + shift) % count)
                for place in range(count)
                if first <= (place + shift) % count < first + total
            ]
            chunk = lax.ppermute(chunk, "wide", pairs)
        received.append(chunk)
    return jnp.stack(received)


def from_groups(blocks, first, total, rank, count):
    received = []
    for shift in range(count):
        block = blocks[shift]
        if shift:
            pairs = [(place, (place - shift) % count) for place in range(first, first + total)]
            block = lax.ppermute(block, "wide", pairs)
        received.append(block)
    stacked = jnp.stack(received)
    return [
        lax.dynamic_index_in_dim(stacked, (first + k - rank) % count, 0, keepdims=False)
        for k in range(total)
    ]


def exchange(blocks):
    return lax.all_to_all(blocks, "wide", 0, 0, tiled=True)


def small_dot(left, right):
    return jnp.dot(
        left.astype(jnp.bfloat16), right.astype(jnp.bfloat16), preferred_element_type=jnp.float32
    )


def orthogonal_factor(gram):
    side = gram.shape[0]
    eye = jnp.eye(side, dtype=jnp.float32)
    factor = None
    for sweep in range(SWEEPS):
        mean = jnp.sum(gram * eye) / side
        rest = gram - mean * eye
        squared = small_dot(rest, rest)
        lead = COEF_LINEAR + COEF_CUBIC * mean + COEF_QUINTIC * mean * mean
        step = (COEF_CUBIC + 2.0 * COEF_QUINTIC * mean) * rest + COEF_QUINTIC * squared
        if sweep + 1 < SWEEPS:
            half = lead * gram + small_dot(gram, step)
            gram = lead * half + small_dot(half, step)
        if factor is None:
            factor = lead * eye + step
        else:
            factor = lead * factor + small_dot(factor, step)
    return factor


def shards(
    inputs,
    out_grad,
    qkv_w,
    out_w,
    ffn_in,
    ffn_out,
    qkv_mom,
    out_mom,
    in_mom,
    down_mom,
    gains,
    gains_m,
    gains_v,
    fgate_w,
    fgate_w_m,
    fgate_w_v,
    fgate_b,
    fgate_b_m,
    fgate_b_v,
    doc_ids,
    group_ids,
    block_mask,
):
    rank = lax.axis_index("wide")
    wide_count = lax.axis_size("wide")
    narrow_count = lax.axis_size("narrow")
    tokens = inputs.shape[1]
    seq_len = doc_ids.shape[1]
    slots = group_ids.shape[1]
    heads = -(-H // wide_count)
    head_cols = heads * DH
    padded = wide_count * head_cols
    in_rows = qkv_w.shape[1]
    ff_rows = ffn_out.shape[0]
    part_rows = D // wide_count
    scale = DH ** (-0.5)
    bf = jnp.bfloat16
    f32 = jnp.float32

    def own_tokens(array):
        return lax.dynamic_slice_in_dim(array, rank * tokens, tokens, 0)

    all_inputs = lax.all_gather(inputs[0], "wide", axis=0, tiled=True)
    qkv_cut = jnp.pad(qkv_w.astype(bf), ((0, 0), (0, 0), (0, padded - D)))
    qkv_cut = qkv_cut.reshape(3, in_rows, wide_count, head_cols).transpose(2, 0, 1, 3)
    qkv_cut = exchange(qkv_cut)
    qkv_all = lax.all_gather(qkv_cut, "narrow", axis=1)
    w_qkv = qkv_all.transpose(0, 1, 3, 2, 4).reshape(D, 3 * head_cols)
    w_out = lax.all_gather(out_w.astype(bf), ("wide", "narrow"), axis=0, tiled=True)
    w_in = lax.all_gather(ffn_in.astype(bf), "narrow", axis=2, tiled=True)
    w_down = lax.all_gather(ffn_out.astype(bf), "narrow", axis=0, tiled=True)
    all_out_grad = lax.all_gather(out_grad[0], "wide", axis=0, tiled=True)

    padding = padded // DH - H
    gate_w = lax.dynamic_slice_in_dim(
        jnp.pad(fgate_w.astype(bf), ((0, 0), (0, padding))), rank * heads, heads, 1
    )
    gate_b = lax.dynamic_slice_in_dim(jnp.pad(fgate_b, ((0, padding),)), rank * heads, heads, 0)

    slot_ids = group_ids[0]
    within = jnp.arange(CH, dtype=jnp.int32)
    place = (slot_ids[:, None] * CH + within[None, :]).reshape(seq_len)
    row_slot = jnp.repeat(slot_ids, CH)
    one_hot = (row_slot[:, None] == jnp.arange(slots)[None, :]).astype(bf)
    slot_hot = (slot_ids[:, None] == jnp.arange(slots)[None, :]).astype(bf)
    docs = jnp.dot(
        slot_hot, doc_ids[0].reshape(slots, CH).astype(bf), preferred_element_type=f32
    ).reshape(seq_len)
    allowed = jnp.eye(slots, dtype=bf) + (block_mask[0] == 1).astype(bf)
    row_allow = jnp.dot(one_hot, allowed, preferred_element_type=f32).astype(bf)
    same_doc = docs[:, None] == docs[None, :]
    before = same_doc & (place[None, :] <= place[:, None])
    before_f = before.astype(bf)

    resid = all_inputs.astype(f32)
    normed_one, _ = rms_parts(resid)
    attn_in = (normed_one * gains[0]).astype(bf)
    projected = jnp.dot(attn_in, w_qkv, preferred_element_type=f32).astype(bf)
    q_heads, k_heads, v_heads = (
        projected[:, k * head_cols : (k + 1) * head_cols]
        .reshape(seq_len, heads, DH)
        .transpose(1, 0, 2)
        for k in range(3)
    )
    logits = jnp.dot(attn_in, gate_w, preferred_element_type=f32) + gate_b
    log_forget = jax.nn.log_sigmoid(logits)
    cumulative = open_sum(before_f, log_forget)
    cum_cols = cumulative.T

    block = min(seq_len, 1024)

    def masked_scores(first):
        rows = slice(first, first + block)
        ok = before[rows] & (
            jnp.dot(row_allow[rows], one_hot.T, preferred_element_type=f32) > 0.5
        )
        raw = jnp.einsum("hid,hjd->hij", q_heads[:, rows], k_heads, preferred_element_type=f32)
        scores = raw * scale + cum_cols[:, rows, None] - cum_cols[:, None, :]
        return jnp.where(ok[None], scores, MASKED_SCORE)

    attended, totals = [], []
    for first in range(0, seq_len, block):
        scores = masked_scores(first)
        top = jnp.max(scores, axis=2, keepdims=True)
        weights = jnp.exp(scores - top)
        total = jnp.sum(weights, axis=2, keepdims=True)
        added = jnp.einsum("hij,hjd->hid", weights.astype(bf), v_heads, preferred_element_type=f32)
        attended.append(added / total)
        totals.append(top + jnp.log(total))
    attended = jnp.concatenate(attended, axis=1)
    log_total = jnp.concatenate(totals, axis=1)
    mixed_own = attended.astype(bf).transpose(1, 0, 2).reshape(seq_len, head_cols)
    mixed = lax.all_gather(mixed_own, "wide", axis=1, tiled=True)[:, :D]
    middle = resid + jnp.dot(mixed, w_out, preferred_element_type=f32)
    normed_two, _ = rms_parts(middle)
    ffn_input = (normed_two * gains[1]).astype(bf)
    gate_value = jnp.dot(ffn_input, w_in[0], preferred_element_type=f32)
    up_value = jnp.dot(ffn_input, w_in[1], preferred_element_type=f32)
    gate_sigmoid = jax.nn.sigmoid(gate_value)
    hidden = (gate_value * gate_sigmoid * up_value).astype(bf)

    grad_hidden = matmul_last(all_out_grad, w_down).astype(bf).astype(f32)
    grad_gate = grad_hidden * up_value * gate_sigmoid * (1.0 + gate_value * (1.0 - gate_sigmoid))
    grad_gate = grad_gate.astype(bf)
    grad_up = (grad_hidden * gate_value * gate_sigmoid).astype(bf)
    part_two = matmul_last(grad_gate, w_in[0]) + matmul_last(grad_up, w_in[1])
    grad_two = lax.psum_scatter(
        part_two.astype(bf), "wide", scatter_dimension=0, tiled=True
    ).astype(f32)
    middle_own = own_tokens(middle)
    normed_own, factor_own = rms_parts(middle_own)
    gain_two = jnp.sum(grad_two * normed_own, axis=0)
    grad_middle = out_grad[0].astype(f32) + rms_back(grad_two, gains[1], normed_own, factor_own)
    grad_branch = lax.all_gather(grad_middle.astype(bf), "wide", axis=0, tiled=True)

    out_part = jnp.dot(hidden, w_down, preferred_element_type=f32)
    result = middle_own + lax.psum_scatter(
        out_part.astype(bf), "wide", scatter_dimension=0, tiled=True
    ).astype(f32)

    d_down = matmul_first(hidden, all_out_grad)
    d_in = jnp.stack([matmul_first(ffn_input, grad_gate), matmul_first(ffn_input, grad_up)])
    mixed_part = lax.dynamic_slice_in_dim(mixed, rank * part_rows, part_rows, 1)
    d_out = matmul_first(mixed_part, grad_branch)

    w_out_own = lax.dynamic_slice_in_dim(
        jnp.pad(w_out, ((0, padded - D), (0, 0))), rank * head_cols, head_cols, 0
    )
    grad_mixed = (
        matmul_last(grad_branch, w_out_own).astype(bf).reshape(seq_len, heads, DH).transpose(1, 0, 2)
    )
    delta = jnp.sum(grad_mixed.astype(f32) * attended, axis=2, keepdims=True)
    grad_q, cum_q = [], []
    grad_k = jnp.zeros((heads, seq_len, DH), f32)
    grad_v = jnp.zeros((heads, seq_len, DH), f32)
    cum_k = jnp.zeros((heads, seq_len), f32)
    for first in range(0, seq_len, block):
        rows = slice(first, first + block)
        probs = jnp.exp(masked_scores(first) - log_total[:, rows])
        dprobs = jnp.einsum(
            "hid,hjd->hij", grad_mixed[:, rows], v_heads, preferred_element_type=f32
        )
        dscores = (probs * (dprobs - delta[:, rows])).astype(bf)
        grad_q.append(
            jnp.einsum("hij,hjd->hid", dscores, k_heads, preferred_element_type=f32) * scale
        )
        grad_k += (
            jnp.einsum("hij,hid->hjd", dscores, q_heads[:, rows], preferred_element_type=f32)
            * scale
        )
        grad_v += jnp.einsum(
            "hij,hid->hjd", probs.astype(bf), grad_mixed[:, rows], preferred_element_type=f32
        )
        cum_q.append(jnp.sum(dscores.astype(f32), axis=2))
        cum_k += jnp.sum(dscores.astype(f32), axis=1)
    cum_grad = (jnp.concatenate(cum_q, axis=1) - cum_k).T
    grad_log = open_sum(before_f.T, cum_grad)
    grad_logit = (grad_log * jax.nn.sigmoid(-logits)).astype(bf)
    grad_proj = jnp.concatenate(
        [
            member.astype(bf).transpose(1, 0, 2).reshape(seq_len, head_cols)
            for member in (jnp.concatenate(grad_q, axis=1), grad_k, grad_v)
        ],
        axis=1,
    )
    d_qkv = matmul_first(attn_in, grad_proj)
    d_forget_w = matmul_first(attn_in, grad_logit)
    d_forget_b = jnp.sum(grad_logit.astype(f32), axis=0)
    part_one = matmul_last(grad_proj, w_qkv) + matmul_last(grad_logit, gate_w)
    gain_one = jnp.sum(part_one * normed_one, axis=0)
    grad_one = lax.psum_scatter(
        part_one.astype(bf), "wide", scatter_dimension=0, tiled=True
    ).astype(f32)
    first_own, first_factor = rms_parts(inputs[0].astype(f32))
    grad_input = grad_middle + rms_back(grad_one, gains[0], first_own, first_factor)

    red_down = lax.psum_scatter(d_down, "narrow", scatter_dimension=0, tiled=True)
    red_in = lax.psum_scatter(d_in, "narrow", scatter_dimension=2, tiled=True)
    red_out = lax.psum_scatter(d_out, "narrow", scatter_dimension=0, tiled=True)
    red_qkv = lax.psum_scatter(
        d_qkv.reshape(wide_count, narrow_count, in_rows, 3 * head_cols),
        "narrow",
        scatter_dimension=1,
        tiled=True,
    ).reshape(wide_count, in_rows, 3, head_cols)
    sum_gate_w, sum_gate_b = lax.psum((d_forget_w, d_forget_b), "narrow")
    sum_gains = lax.psum(jnp.stack([gain_one, gain_two]), ("wide", "narrow"))
    local_square = (
        jnp.sum(red_qkv * red_qkv)
        + jnp.sum(red_out * red_out)
        + jnp.sum(red_in * red_in)
        + jnp.sum(red_down * red_down)
        + (jnp.sum(sum_gate_w * sum_gate_w) + jnp.sum(sum_gate_b * sum_gate_b)) / narrow_count
    )
    square_total = lax.psum(local_square, ("wide", "narrow")) + jnp.sum(sum_gains * sum_gains)
    grad_norm = jnp.sqrt(square_total)
    clip_factor = jnp.minimum(1.0, CLIP_NORM / (grad_norm + 1e-06))

    gate_w_all = lax.all_gather(sum_gate_w, "wide", axis=1, tiled=True)[:, :H]
    gate_b_all = lax.all_gather(sum_gate_b, "wide", axis=0, tiled=True)[:H]

    own_qkv = (
        exchange(red_qkv).transpose(2, 1, 0, 3).reshape(3, in_rows, padded)[:, :, :D]
    )

    spare = wide_count - 4
    small_moms = exchange(
        jnp.concatenate(
            [qkv_mom.astype(bf), out_mom.astype(bf)[None], jnp.zeros((spare, in_rows, D), bf)]
        )
    )
    ff_moms = to_groups(
        jnp.stack([in_mom[0].astype(bf).T, in_mom[1].astype(bf).T, down_mom.astype(bf)]),
        4,
        rank,
        wide_count,
    )
    out_grads = exchange(
        jnp.concatenate(
            [
                jnp.zeros((3, in_rows, D), bf),
                red_out.astype(bf)[None],
                jnp.zeros((spare, in_rows, D), bf),
            ]
        )
    )
    ff_grads = to_groups(
        jnp.stack([red_in[0].astype(bf).T, red_in[1].astype(bf).T, red_down.astype(bf)]),
        4,
        rank,
        wide_count,
    )
    qkv_grads = exchange(
        jnp.concatenate(
            [
                red_qkv.astype(bf)
                .transpose(2, 0, 1, 3)
                .reshape(3, wide_count * in_rows, head_cols),
                jnp.zeros((spare + 1, wide_count * in_rows, head_cols), bf),
            ]
        )
    )
    qkv_grads = qkv_grads.transpose(1, 0, 2).reshape(wide_count * in_rows, padded)[:, :D]
    small_own = jnp.where(rank == 3, out_grads.reshape(-1, D), qkv_grads)
    small_mom_own = small_moms.reshape(-1, D)
    ff_own = ff_grads.reshape(-1, D)
    ff_mom_own = ff_moms.reshape(-1, D)
    small_all = lax.all_gather(small_own, "narrow", axis=0, tiled=True)
    small_mom_all = lax.all_gather(small_mom_own, "narrow", axis=0, tiled=True)
    ff_all = lax.all_gather(ff_own, "narrow", axis=0, tiled=True)
    ff_mom_all = lax.all_gather(ff_mom_own, "narrow", axis=0, tiled=True)

    lead_coef = (1.0 + MOMENTUM) * clip_factor
    mom_coef = MOMENTUM * MOMENTUM

    def direction(gradient, moment):
        return (lead_coef * gradient.astype(f32) + mom_coef * moment.astype(f32)).astype(bf)

    holds_ff = (rank >= 4) & (rank < 7)

    def ff_gram(operands):
        rows = direction(operands[2], operands[3])
        return matmul_first(rows, rows)

    def small_gram(operands):
        rows = direction(operands[0], operands[1])
        return matmul_first(rows, rows)

    gram = lax.cond(
        holds_ff, ff_gram, small_gram, (small_all, small_mom_all, ff_all, ff_mom_all)
    )
    norm_square = jnp.sum(gram * jnp.eye(D, dtype=f32))
    inverse = 1.0 / (jnp.sqrt(norm_square) + 1e-07)
    factor = (orthogonal_factor(gram * (inverse * inverse)) * inverse).astype(bf)
    small_ortho = jnp.dot(
        direction(small_own, small_mom_own), factor, preferred_element_type=f32
    ).astype(bf)
    ff_ortho = jnp.dot(
        direction(ff_own, ff_mom_own), factor, preferred_element_type=f32
    ).astype(bf)
    small_back = exchange(small_ortho.reshape(wide_count, in_rows, D))
    ff_back = from_groups(ff_ortho.reshape(wide_count, ff_rows, D), 4, 3, rank, wide_count)
    ortho_qkv = small_back[0:3].astype(f32)
    ortho_out = small_back[3].astype(f32)
    ortho_in = jnp.stack([ff_back[0].T, ff_back[1].T]).astype(f32)
    ortho_down = ff_back[2].astype(f32)

    def moved(moment, gradient):
        return MOMENTUM * moment + clip_factor * gradient

    def stepped(weight, rate, ortho):
        return (1.0 - MUON_DECAY) * weight - rate * ortho

    bias_one = 1.0 - BETA_FIRST**STEP
    bias_two = 1.0 - BETA_SECOND**STEP
    gains_new, gains_first, gains_second = adam_update(
        gains, gains_m, gains_v, clip_factor * sum_gains, bias_one, bias_two, RATE_GAINS
    )
    forget_w_new, forget_w_first, forget_w_second = adam_update(
        fgate_w, fgate_w_m, fgate_w_v, clip_factor * gate_w_all, bias_one, bias_two, RATE_FGATE_W
    )
    forget_b_new, forget_b_first, forget_b_second = adam_update(
        fgate_b, fgate_b_m, fgate_b_v, clip_factor * gate_b_all, bias_one, bias_two, RATE_FGATE_B
    )
    return (
        result.astype(bf)[None],
        grad_input[None],
        grad_norm.reshape(1),
        stepped(qkv_w, tall_rate(D, D, D), ortho_qkv),
        stepped(out_w, tall_rate(D, D, D // 32), ortho_out),
        stepped(ffn_in, tall_rate(FF, D, D), ortho_in),
        stepped(ffn_out, tall_rate(FF, D, FF), ortho_down),
        moved(qkv_mom, own_qkv),
        moved(out_mom, red_out),
        moved(in_mom, red_in),
        moved(down_mom, red_down),
        gains_new,
        gains_first,
        gains_second,
        forget_w_new,
        forget_w_first,
        forget_w_second,
        forget_b_new,
        forget_b_first,
        forget_b_second,
    )


def solution(mesh):
    placed = (
        P("narrow", "wide", None),
        P("narrow", "wide", None),
        P(None, ("wide", "narrow"), None),
        P(("wide", "narrow"), None),
        P(None, None, ("wide", "narrow")),
        P(("wide", "narrow"), None),
        P(None, ("wide", "narrow"), None),
        P(("wide", "narrow"), None),
        P(None, None, ("wide", "narrow")),
        P(("wide", "narrow"), None),
        P(),
        P(),
        P(),
        P(),
        P(),
        P(),
        P(),
        P(),
        P(),
        P("narrow", None),
        P("narrow", None),
        P("narrow", None, None),
    )
    return jax.shard_map(
        shards,
        mesh=mesh,
        in_specs=placed,
        out_specs=(
            P("narrow", "wide", None),
            P("narrow", "wide", None),
            P(),
            P(None, ("wide", "narrow"), None),
            P(("wide", "narrow"), None),
            P(None, None, ("wide", "narrow")),
            P(("wide", "narrow"), None),
            P(None, ("wide", "narrow"), None),
            P(("wide", "narrow"), None),
            P(None, None, ("wide", "narrow")),
            P(("wide", "narrow"), None),
            P(),
            P(),
            P(),
            P(),
            P(),
            P(),
            P(),
            P(),
            P(),
        ),
        check_vma=False,
    )
```

time: 6360 us -> 1680 us (0.26)
  waiting for transfers between devices: 4790 us -> 784 us
  local copies, waits for them, and re-layouts: 564 us -> 56.6 us
  matrix products: 551 us -> 394 us
  other arithmetic: 199 us -> 69.9 us
  starting transfers between devices: 5.26 us -> 121 us
  blocking collectives: 137 us -> 204 us
  loops' own time: 66.8 us -> 0.15 us
    all_gather x50 -> x12, waiting for transfers between devices: 2140 us -> 424 us  [the longest x1 83.8 us: shards(): ff_all = lax.all_gather(ff_own, 'narrow', axis=0, tiled=True)]
    psum x10 -> x0, waiting for transfers between devices: 1520 us -> none  [the longest x5 765 us: shards(): lax.psum((halves[0], halves[1], halves[2], halves[3], halves[4], halves[5...]
    reduce_scatter x3 -> x6, waiting for transfers between devices: 678 us -> 165 us  [the longest x1 72.6 us: shards(): lax.psum_scatter(part_two.astype(bf), 'wide', scatter_dimension=0, tiled=...]
    unnamed x65 -> x20, waiting for transfers between devices: 456 us -> 43 us
    dot_general x74 -> x7, matrix products: 304 us -> 39.8 us  [matmul_first(): lax.dot_general(left, right, (((0,), (0,)), ((), ())), preferred_element_...]
    dynamic_slice x239 -> x1, local copies, waits for them, and re-layouts: 182 us -> 0.07 us  [shards(): lax.dynamic_slice_in_dim(jnp.pad(fgate_b, ((0, padding),)), rank * heads,...]
    gather x93 -> x0, local copies, waits for them, and re-layouts: 125 us -> none  [the longest x32 41.3 us: key_mask(): group_ok = jnp.take(allow_pair, key_group, axis=1)]
    dot_general x107 -> x34, matrix products: 208 us -> 332 us  [the longest x16 262 us: small_dot(): jnp.dot(left.astype(jnp.bfloat16), right.astype(jnp.bfloat16), preferred_...]
  transfers between devices with their start and end apart: 64 -> 44, of which waited for: 58 -> 21; matrix products, arithmetic and copies ran while one was open for 17% -> 10% of each run, Pallas kernels for 0% -> 0%
where the time goes in v1:
time: 1680 us; the launch traced here: 1670 us
  waiting for transfers between devices  784 us (47%)
  matrix products  394 us (23%)
  blocking collectives  204 us (12%)
  starting transfers between devices  121 us (7%)
  other arithmetic  69.9 us (4%)
  local copies, waits for them, and re-layouts  56.6 us (3%)
  between operations  39.8 us (2%)
    dot_general x16, matrix products, small_dot(): jnp.dot(left.astype(jnp.bfloat16), right.astype(jnp.bfloat16), preferred_...  262 us
    ppermute x7, waiting for transfers between devices, from_groups(): block = lax.ppermute(block, 'wide', pairs)  89.2 us
    all_gather x1, waiting for transfers between devices, shards(): ff_all = lax.all_gather(ff_own, 'narrow', axis=0, tiled=True)  83.8 us
    all_to_all x2, blocking collectives, exchange(): return lax.all_to_all(blocks, 'wide', 0, 0, tiled=True)  79.8 us
    ppermute x14, starting transfers between devices, to_groups(): chunk = lax.ppermute(chunk, 'wide', pairs)  74.9 us
    reduce_scatter x1, waiting for transfers between devices, shards(): lax.psum_scatter(part_two.astype(bf), 'wide', scatter_dimension=0, tiled=...  72.6 us
    all_gather x1, waiting for transfers between devices, shards(): mixed = lax.all_gather(mixed_own, 'wide', axis=1, tiled=True)[:, :D]  61.9 us
    all_gather x1, waiting for transfers between devices, shards(): lax.all_gather(out_w.astype(bf), ('wide', 'narrow'), axis=0, tiled=True)  60.5 us
  transfers between devices with their start and end apart: 44, of which 21 were waited for; matrix products, arithmetic and copies ran while one was open for 10% of the time, Pallas kernels for 0%

profile of v1, /device:TPU:0, one launch (start us, length us, event | category | flops | bytes accessed | tf_op | source)
XLA Modules:
  0.0 1670.4 jit_solution(8798674172923413453)
XLA Ops:
  9.2 23.6 %all_to_all.30 = bf16[8,3,48,192]{3,2,1,0:T(8,128)(2,1)S(1)} all-to-all(bf16[8,3,48,192]{3,2,1,0:T(8,128)(2,1)S(1)} %copy.114), channel_id=1, replica_groups=mesh['wide'=8,'narrow'=4] {'wide'}, dimensions={0} | all-to-all | bytes 884736 | tf_op jit(solution)/shard_map/all_to_all | solution.py:112
  41.9 14.4 all-gather.37.cloned.1.call-done
  63.9 55.1 %all-gather.35.cloned.1.call-done = bf16[1,1024,1536]{2,1,0:T(8,128)(2,1)} async-done(((bf16[1,128,1536]{2,1,0:T(8,128)(2,1)}), bf16[1,1024,1536]{2,1,0:T(8,128)(2,1)}) %all-gather.35.cloned.1.call-update) | async-done | bytes 3145744 | tf_op jit(solution)/shard_map/all_gather | solution.py:184
  142.8 59.2 %all-gather.39.cloned.1.call-done = bf16[1,1024,1536]{2,1,0:T(8,128)(2,1)} async-done(((bf16[1,128,1536]{2,1,0:T(8,128)(2,1)}), bf16[1,1024,1536]{2,1,0:T(8,128)(2,1)}) %all-gather.39.cloned.1.call-update) | async-done | bytes 3145744 | tf_op jit(solution)/shard_map/all_gather | solution.py:193
  202.0 5.1 fusion.82
  207.1 60.5 %all-gather.19.cloned.1.call-done = bf16[1536,1536]{1,0:T(8,128)(2,1)} async-done(((bf16[48,1536]{1,0:T(8,128)(2,1)}), bf16[1536,1536]{1,0:T(8,128)(2,1)}) %all-gather.19.cloned.1.call-update) | async-done | bytes 4718608 | tf_op jit(solution)/shard_map/all_gather | solution.py:190
  267.6 61.9 %all-gather.17.cloned.1.call-done = bf16[1024,1536]{0,1:T(8,128)(2,1)} async-done(((bf16[1024,192]{0,1:T(8,128)(2,1)}), bf16[1024,1536]{0,1:T(8,128)(2,1)}) %all-gather.17.cloned.1.call-update) | async-done | bytes 3145744 | tf_op jit(solution)/shard_map/all_gather | solution.py:254
  329.5 8.5 multiply_reduce_fusion
  343.0 16.2 all-gather.21.cloned.1.call-done
  359.2 4.3 fusion.86
  375.7 72.6 %reduce-scatter.10.cloned.1.call-done = bf16[128,1536]{1,0:T(8,128)(2,1)} async-done(((bf16[1024,1536]{1,0:T(8,128)(2,1)}), bf16[128,1536]{1,0:T(8,128)(2,1)}) %reduce-scatter.10.cloned.1.call-update) | async-done | bytes 393232 | tf_op jit(solution)/shard_map/reduce_scatter | solution.py:268
  455.1 57.9 %all-gather.25.cloned.1.call-done = bf16[1024,1536]{1,0:T(8,128)(2,1)} async-done(((bf16[128,1536]{1,0:T(8,128)(2,1)}), bf16[1024,1536]{1,0:T(8,128)(2,1)}) %all-gather.25.cloned.1.call-update) | async-done | bytes 3145744 | tf_op jit(solution)/shard_map/all_gather | solution.py:275
  516.2 6.7 fusion.90
  523.1 7.5 convert_reduce_fusion
  534.0 4.9 fusion.111
  539.0 5.7 fusion.59
  562.4 4.5 fusion.112
  572.0 5.3 convolution_convert_fusion.1
  577.4 41.5 %all-reduce.7.cloned.1.call-done = f32[8,4,48,576]{3,2,1,0:T(8,128)} async-done(((f32[8,4,48,576]{3,2,1,0:T(8,128)}), f32[8,4,48,576]{3,2,1,0:T(8,128)}) %all-reduce.7.cloned.1.call-update) | async-done | bytes 3538960
  623.6 5.5 all-to-all-start.5
  629.7 29.9 %reduce-scatter.18.cloned.1.call-done = f32[128,1536]{0,1:T(8,128)} async-done(((f32[512,1536]{0,1:T(8,128)}), f32[128,1536]{0,1:T(8,128)}) %reduce-scatter.18.cloned.1.call-update) | async-done | bytes 786448 | tf_op jit(solution)/shard_map/reduce_scatter | solution.py:338
  664.3 10.3 all-reduce.4
  677.2 43.4 %reduce-scatter.16.cloned.1.call-done = f32[2,1536,128]{2,1,0:T(8,128)} async-done(((f32[2,1536,512]{2,1,0:T(8,128)}), f32[2,1536,128]{2,1,0:T(8,128)}) %reduce-scatter.16.cloned.1.call-update) | async-done | bytes 1572880 | tf_op jit(solution)/shard_map/reduce_scatter | solution.py:339
  724.7 5.5 all-to-all-start.2
  730.2 19.2 %reduce-scatter.14.cloned.1.call-done = f32[48,1536]{1,0:T(8,128)} async-done(((f32[192,1536]{1,0:T(8,128)}), f32[48,1536]{1,0:T(8,128)}) %reduce-scatter.14.cloned.1.call-update) | async-done | bytes 294928 | tf_op jit(solution)/shard_map/reduce_scatter | solution.py:340
  753.7 41.6 %all-reduce.3 = (f32[]{:T(128)}, f32[2,1536]{1,0:T(2,128)S(1)}) all-reduce(f32[]{:T(128)S(6)} %add.495, f32[2,1536]{1,0:T(2,128)S(1)} %pad_maximum_fusion.6), channel_id=1, replica_groups=mesh['wide'=8,'narrow'=4] {'wide','narrow'}, use_global_device_ids=true, to_apply=%region_27.28 | all-reduce | flops 3073 | bytes 24584 | tf_op jit(solution)/shard_map/psum | solution.py:356
  804.1 5.5 all-to-all-start.1
  811.1 39.4 %all-to-all-done.1 = bf16[8,48,1536]{2,1,0:T(8,128)(2,1)} async-done(((bf16[8,48,1536]{2,1,0:T(8,128)(2,1)}), bf16[8,48,1536]{2,1,0:T(8,128)(2,1)}, u32[]{:S(2)}, u32[]{:S(2)}) %all-to-all-start.1) | async-done | bytes 1179680 | tf_op jit(solution)/shard_map/all_to_all | solution.py:112
  853.4 56.2 %all_to_all.31 = bf16[8,48,1536]{2,1,0:T(8,128)(2,1)} all-to-all(bf16[8,48,1536]{2,1,0:T(8,128)(2,1)S(1)} %get-tuple-element.221), channel_id=1, replica_groups=mesh['wide'=8,'narrow'=4] {'wide'}, dimensions={0} | all-to-all | bytes 2359296 | tf_op jit(solution)/shard_map/all_to_all | solution.py:112
  913.3 6.4 collective-permute-start.10
  921.6 6.4 collective-permute-start.12
  932.0 5.6 collective-permute-done.11
  938.4 5.9 collective-permute-done.12
  953.6 48.7 %collective-permute-start.3 = (bf16[128,1536]{0,1:T(8,128)(2,1)S(1)}, bf16[128,1536]{0,1:T(8,128)(2,1)S(1)}, u32[]{:S(2)}, u32[]{:S(2)}) collective-permute-start(bf16[128,1536]{0,1:T(8,128)(2,1)S(1)} %get-tuple-element.197), channel_id=1, source_target_pairs={{0,16},{4,20},{8,24},{1,17},{5,21},{9,25},{2,18},{6,22},{10,26},{3... | collective-permute-start | bytes 1179656 | tf_op jit(solution)/shard_map/ppermute | solution.py:91
  1012.6 7.6 collective-permute-done.4
  1026.7 4.8 copy.128
  1036.1 41.4 %all-reduce.1 = f32[24]{0:T(128)S(1)} all-reduce(f32[24]{0:T(128)S(1)} %dynamic-update-slice), channel_id=1, replica_groups=mesh['wide'=8,'narrow'=4] {'wide'}, use_global_device_ids=true, to_apply=%add.1 | all-reduce | flops 24 | bytes 192
  1077.6 30.8 %all-gather.3 = f32[8,3,1536]{2,1,0:T(4,128)S(1)} all-gather(f32[1,3,1536]{2,1,0:T(4,128)} %bitcast.321), channel_id=1, replica_groups=mesh['wide'=8,'narrow'=4] {'wide'}, dimensions={0}, use_global_device_ids=true | all-gather | bytes 165888 | tf_op jit(solution)/shard_map/all_gather | solution.py:360
  1118.3 14.7 all-gather.33.cloned.1.call-done
  1133.0 83.8 %all-gather.31.cloned.1.call-done = bf16[4096,1536]{1,0:T(8,128)(2,1)} async-done(((bf16[1024,1536]{1,0:T(8,128)(2,1)}), bf16[4096,1536]{1,0:T(8,128)(2,1)}) %all-gather.31.cloned.1.call-update) | async-done | bytes 12582928 | tf_op jit(solution)/shard_map/all_gather | solution.py:411
  1216.8 16.6 conditional.1
  1216.8 16.4 fusion
  1233.4 4.5 select_reduce_fusion.5
  1238.6 4.5 select_reduce_fusion.4
  1246.3 17.6 %multiply_add_fusion.10 = f32[1536,1536]{1,0:T(8,128)} fusion(f32[1536,1536]{1,0:T(8,128)} %get-tuple-element.240, f32[]{:T(128)S(6)} %div.118, f32[]{:T(128)S(6)} %add.517, f32[]{:T(128)S(6)} %mul.751), kind=kOutput, calls=%fused_computation.51 | convolution fusion | flops 7276068864 | bytes 18874380 | tf_op jit(solution)/shard_map/dot_general | solution.py:116
  1264.0 16.8 %multiply_add_fusion.11 = f32[1536,1536]{1,0:T(8,128)} fusion(f32[1536,1536]{1,0:T(8,128)} %get-tuple-element.240, f32[]{:T(128)S(6)} %add.516, f32[]{:T(128)S(6)} %mul.751, f32[1536,1536]{1,0:T(8,128)} %multiply_add_fusion.10), kind=kOutput, calls=%fused_computation.53 | convolution fusion | flops 7261913088 | bytes 28311560 | tf_op jit(solution)/shard_map/dot_general | solution.py:116
  1280.7 16.9 %select_reduce_fusion.3 = (f32[]{:T(128)}, f32[1536,1536]{1,0:T(8,128)}) fusion(f32[1536,1536]{1,0:T(8,128)S(1)} %copy-done.71, f32[1536,1536]{1,0:T(8,128)} %multiply_add_fusion.11, f32[]{:T(128)S(6)} %add.516), kind=kOutput, calls=%fused_computation.49 | convolution fusion | flops 7264272384 | bytes 28311560 | tf_op jit(solution)/shard_map/dot_general | solution.py:116
  1300.9 16.0 add_convert_fusion.7
  1316.9 15.8 multiply_add_fusion.2
  1332.7 9.8 multiply_add_fusion.8
  1342.6 16.8 %select_reduce_fusion.2 = (f32[]{:T(128)}, f32[1536,1536]{1,0:T(8,128)}) fusion(bf16[1536,1536]{1,0:T(8,128)(2,1)S(1)} %add_convert_fusion.7, f32[1536,1536]{1,0:T(8,128)} %multiply_add_fusion.8, f32[]{:T(128)S(6)} %add.522), kind=kOutput, calls=%fused_computation.44 | convolution fusion | flops 7261913088 | bytes 23592968 | tf_op jit(solution)/shard_map/dot_general | solution.py:116
  1362.6 20.1 %add_convert_fusion.6 = bf16[1536,1536]{1,0:T(8,128)(2,1)} fusion(f32[1536,1536]{1,0:T(8,128)} %get-tuple-element.235, f32[]{:T(128)S(6)} %div.120, f32[]{:T(128)S(6)} %add.529), kind=kOutput, calls=%fused_computation.41 | convolution fusion | flops 7273709568 | bytes 14155784 | tf_op jit(solution)/shard_map/dot_general | solution.py:116
  1382.7 12.2 multiply_add_fusion.6
  1394.9 16.7 select_reduce_fusion.1
  1414.8 19.9 %add_convert_fusion.5 = bf16[1536,1536]{1,0:T(8,128)(2,1)} fusion(f32[1536,1536]{1,0:T(8,128)} %get-tuple-element.237, f32[]{:T(128)S(6)} %div.121, f32[]{:T(128)S(6)} %add.535), kind=kOutput, calls=%fused_computation.36 | convolution fusion | flops 7273709568 | bytes 14155784 | tf_op jit(solution)/shard_map/dot_general | solution.py:116
  1434.8 12.2 multiply_add_fusion.4
  1447.0 16.7 select_reduce_fusion
  1466.9 14.3 multiply_add_fusion.1
  1481.2 11.9 multiply_add_fusion
  1493.1 28.6 %multiply_convert_fusion.1 = bf16[1536,1536]{1,0:T(8,128)(2,1)} fusion(f32[1536,1536]{1,0:T(8,128)} %multiply_add_fusion, f32[]{:T(128)S(6)} %div.117, f32[]{:T(128)S(6)} %add.540, f32[1536,1536]{1,0:T(8,128)} %get-tuple-element.239, f32[]{:T(128)S(6)} %div.122, f32[]{:T(128)S(6)} %add.545), kind=kOutput, calls=%fused_computation.27 | convolution fusion | flops 14533263360 | bytes 23592976 | tf_op jit(solution)/shard_map/dot_general | solution.py:116
  1521.8 5.5 convolution_convert_fusion.2
  1527.3 7.9 convolution_convert_fusion
  1535.2 21.5 %all-to-all-start.4 = ((bf16[8,48,1536]{2,1,0:T(8,128)(2,1)}), bf16[8,48,1536]{2,1,0:T(8,128)(2,1)}, u32[]{:S(2)}, u32[]{:S(2)}) async-start(bf16[8,48,1536]{2,1,0:T(8,128)(2,1)} %bitcast.313), calls=%async_computation.10 | async-start | bytes 2359296 | tf_op jit(solution)/shard_map/all_to_all | solution.py:112
  1563.9 89.2 %collective-permute-done.17 = bf16[128,1536]{1,0:T(8,128)(2,1)S(1)} collective-permute-done((bf16[128,1536]{1,0:T(8,128)(2,1)S(1)}, bf16[128,1536]{1,0:T(8,128)(2,1)S(1)}, u32[]{:S(2)}, u32[]{:S(2)}) %collective-permute-start.17) | collective-permute-done | bytes 393248 | tf_op jit(solution)/shard_map/ppermute | solution.py:102
  (381 shorter events, 190.4 us)
Async XLA Ops:
  7.2 30.2 %copy-start.62 = (s32[1,16,16]{2,1,0:T(8,128)S(1)}, s32[1,16,16]{2,1,0:T(8,128)}, u32[]{:S(2)}) copy-start(s32[1,16,16]{2,1,0:T(8,128)} %param.45) | copy-start | bytes 3076
  7.2 49.1 %all-gather.37.cloned.1.call-start = ((), (), s32[]{:S(2)}) async-start(), calls=%async_computation.28 | async-start | bytes 2949120 | tf_op jit(solution)/shard_map/all_gather | solution.py:188
  33.7 85.3 %all-gather.35.cloned.1.call-start = ((), (), s32[]{:S(2)}) async-start(), calls=%async_computation.27 | async-start | bytes 3538944 | tf_op jit(solution)/shard_map/all_gather | solution.py:184
  34.5 108.4 %all-gather.23.cloned.1.call-start = ((), (), s32[]{:S(2)}) async-start(), calls=%async_computation.15 | async-start | bytes 1966080 | tf_op jit(solution)/shard_map/all_gather | solution.py:192
  35.3 166.7 %all-gather.39.cloned.1.call-start = ((), (), s32[]{:S(2)}) async-start(), calls=%async_computation.29 | async-start | bytes 3538944 | tf_op jit(solution)/shard_map/all_gather | solution.py:193
  35.9 231.7 %all-gather.19.cloned.1.call-start = ((), (), s32[]{:S(2)}) async-start(), calls=%async_computation.13 | async-start | bytes 4866048 | tf_op jit(solution)/shard_map/all_gather | solution.py:190
  36.7 292.9 %all-gather.17.cloned.1.call-start = ((), (), s32[]{:S(2)}) async-start(), calls=%async_computation.12 | async-start | bytes 3538944 | tf_op jit(solution)/shard_map/all_gather | solution.py:254
  36.9 88.4 %copy-start.52 = (s32[1024]{0:T(1024)}, s32[1024]{0:T(1024)S(1)}, u32[]{:S(2)}) copy-start(s32[1024]{0:T(1024)S(1)} %add.463) | copy-start | bytes 12292
  37.3 88.1 %copy-start.53 = (f32[1024]{0:T(1024)}, f32[1024]{0:T(1024)S(1)}, u32[]{:S(2)}) copy-start(f32[1024]{0:T(1024)S(1)} %eq.108) | copy-start | bytes 12292
  41.9 84.5 %copy-start.41 = (f32[1536]{0:T(1024)}, f32[1536]{0:T(1024)S(1)}, u32[]{:S(2)}) copy-start(f32[1536]{0:T(1024)S(1)} %get-tuple-element.149) | copy-start | bytes 18436
  41.9 296.2 %copy-start.37 = (f32[1536]{0:T(1024)}, f32[1536]{0:T(1024)S(1)}, u32[]{:S(2)}) copy-start(f32[1536]{0:T(1024)S(1)} %get-tuple-element.148) | copy-start | bytes 18436
  140.1 219.2 %all-gather.21.cloned.1.call-start = ((), (), s32[]{:S(2)}) async-start(), calls=%async_computation.14 | async-start | bytes 3932160 | tf_op jit(solution)/shard_map/all_gather | solution.py:191
  142.5 305.8 %reduce-scatter.10.cloned.1.call-start = ((), (), s32[]{:S(2)}) async-start(), calls=%async_computation.17 | async-start | bytes 3538944 | tf_op jit(solution)/shard_map/reduce_scatter | solution.py:268
  373.8 77.2 %copy-start.13 = (bf16[1,128,1536]{2,1,0:T(8,128)(2,1)S(1)}, bf16[1,128,1536]{2,1,0:T(8,128)(2,1)}, u32[]{:S(2)}) copy-start(bf16[1,128,1536]{2,1,0:T(8,128)(2,1)} %param.25) | copy-start | bytes 1179652
  373.8 139.2 %all-gather.25.cloned.1.call-start = ((), (), s32[]{:S(2)}) async-start(), calls=%async_computation.18 | async-start | bytes 3538944 | tf_op jit(solution)/shard_map/all_gather | solution.py:275
  453.3 165.6 %all-reduce.7.cloned.1.call-start = ((), (), s32[]{:S(2)}) async-start(), calls=%async_computation.30 | async-start | bytes 7864320
  538.9 120.6 %reduce-scatter.18.cloned.1.call-start = ((), (), s32[]{:S(2)}) async-start(), calls=%async_computation.22 | async-start | bytes 3932160 | tf_op jit(solution)/shard_map/reduce_scatter | solution.py:338
  544.7 175.8 %reduce-scatter.16.cloned.1.call-start = ((), (), s32[]{:S(2)}) async-start(), calls=%async_computation.21 | async-start | bytes 7864320 | tf_op jit(solution)/shard_map/reduce_scatter | solution.py:339
  554.4 195.0 %reduce-scatter.14.cloned.1.call-start = ((), (), s32[]{:S(2)}) async-start(), calls=%async_computation.20 | async-start | bytes 1474560 | tf_op jit(solution)/shard_map/reduce_scatter | solution.py:340
  558.4 555.8 %reduce-scatter.12.cloned.1.call-start = ((), (), s32[]{:S(2)}) async-start(), calls=%async_computation.19 | async-start | bytes 3538944 | tf_op jit(solution)/shard_map/reduce_scatter | solution.py:332
  571.2 544.3 %reduce-scatter.8.cloned.1.call-start = ((), (), s32[]{:S(2)}) async-start(), calls=%async_computation.16 | async-start | bytes 3538944 | tf_op jit(solution)/shard_map/reduce_scatter | solution.py:278
  621.6 39.9 %copy-start.50 = (f32[1024]{0:T(1024)S(1)}, f32[1024]{0:T(1024)}, u32[]{:S(2)}) copy-start(f32[1024]{0:T(1024)} %copy-done.47) | copy-start | bytes 12292
  623.6 101.2 %all-to-all-start.5 = ((f32[8,48,3,192]{3,1,2,0:T(8,128)}), f32[8,48,3,192]{3,1,2,0:T(8,128)S(1)}, u32[]{:S(2)}, u32[]{:S(2)}) async-start(f32[8,48,3,192]{3,1,2,0:T(8,128)} %copy.131), calls=%async_computation.11 | async-start | bytes 2359296 | tf_op jit(solution)/shard_map/all_to_all | solution.py:112
  674.6 45.9 %copy-start.40 = (f32[1536,3]{0,1:T(4,128)}, f32[1536,3]{0,1:T(4,128)S(1)}, u32[]{:S(2)}) copy-start(f32[1536,3]{0,1:T(4,128)S(1)} %get-tuple-element.152) | copy-start | bytes 55300
  674.6 45.9 %copy-start.63 = (f32[3]{0:T(128)}, f32[3]{0:T(128)S(1)}, u32[]{:S(2)}) copy-start(f32[3]{0:T(128)S(1)} %get-tuple-element.153) | copy-start | bytes 40
  723.0 74.3 %copy-start.36 = (f32[48,1536]{1,0:T(8,128)S(1)}, f32[48,1536]{1,0:T(8,128)}, u32[]{:S(2)}) copy-start(f32[48,1536]{1,0:T(8,128)} %param.31) | copy-start | bytes 884740
  724.7 79.4 %all-to-all-start.2 = ((bf16[8,384,192]{1,2,0:T(8,128)(2,1)}), bf16[8,384,192]{1,2,0:T(8,128)(2,1)S(1)}, u32[]{:S(2)}, u32[]{:S(2)}) async-start(bf16[8,384,192]{1,2,0:T(8,128)(2,1)} %concatenate.24.clone), calls=%async_computation.8 | async-start | bytes 2359296 | tf_op jit(solution)/shard_map/all_to_all | solution.py:112
  804.1 46.4 %all-to-all-start.1 = ((bf16[8,48,1536]{2,1,0:T(8,128)(2,1)}), bf16[8,48,1536]{2,1,0:T(8,128)(2,1)}, u32[]{:S(2)}, u32[]{:S(2)}) async-start(bf16[8,48,1536]{2,1,0:T(8,128)(2,1)} %get-tuple-element.222), calls=%async_computation.7 | async-start | bytes 2359296 | tf_op jit(solution)/shard_map/all_to_all | solution.py:112
  809.6 308.7 %all-gather.27.cloned.1.call-start = ((), (), s32[]{:S(2)}) async-start(), calls=%async_computation.23 | async-start | bytes 5898240 | tf_op jit(solution)/shard_map/all_gather | solution.py:409
  811.1 98.6 %copy-start.5 = (f32[2,1536,128]{2,1,0:T(8,128)S(1)}, f32[2,1536,128]{2,1,0:T(8,128)}, u32[]{:S(2)}) copy-start(f32[2,1536,128]{2,1,0:T(8,128)} %param.32) | copy-start | bytes 4718596
  811.1 98.9 %copy-start.18 = (f32[128,1536]{1,0:T(8,128)S(1)}, f32[128,1536]{1,0:T(8,128)}, u32[]{:S(2)}) copy-start(f32[128,1536]{1,0:T(8,128)} %param.33) | copy-start | bytes 2359300
  853.3 265.0 %all-gather.29.cloned.1.call-start = ((), (), s32[]{:S(2)}) async-start(), calls=%async_computation.24 | async-start | bytes 5898240 | tf_op jit(solution)/shard_map/all_gather | solution.py:410
  909.5 223.5 %all-gather.33.cloned.1.call-start = ((), (), s32[]{:S(2)}) async-start(), calls=%async_computation.26 | async-start | bytes 15728640 | tf_op jit(solution)/shard_map/all_gather | solution.py:412
  911.2 10.3 collective-permute-start.7
  911.9 16.9 %collective-permute-start.8 = (bf16[128,1536]{1,0:T(8,128)(2,1)S(1)}, bf16[128,1536]{1,0:T(8,128)(2,1)S(1)}, u32[]{:S(2)}, u32[]{:S(2)}) collective-permute-start(bf16[128,1536]{1,0:T(8,128)(2,1)S(1)} %get-tuple-element.191), channel_id=1, source_target_pairs={{8,16},{12,20},{16,24},{9,17},{13,21},{17,25},{10,18},{14,22},{18,... | collective-permute-start | bytes 1179656 | tf_op jit(solution)/shard_map/ppermute | solution.py:91
  912.6 17.8 %collective-permute-start.9 = (bf16[128,1536]{1,0:T(8,128)(2,1)S(1)}, bf16[128,1536]{1,0:T(8,128)(2,1)S(1)}, u32[]{:S(2)}, u32[]{:S(2)}) collective-permute-start(bf16[128,1536]{1,0:T(8,128)(2,1)S(1)} %get-tuple-element.190), channel_id=1, source_target_pairs={{4,16},{8,20},{12,24},{5,17},{9,21},{13,25},{6,18},{10,22},{14,26}... | collective-permute-start | bytes 1179656 | tf_op jit(solution)/shard_map/ppermute | solution.py:91
  913.3 17.9 %collective-permute-start.10 = (bf16[128,1536]{1,0:T(8,128)(2,1)S(1)}, bf16[128,1536]{1,0:T(8,128)(2,1)S(1)}, u32[]{:S(2)}, u32[]{:S(2)}) collective-permute-start(bf16[128,1536]{1,0:T(8,128)(2,1)S(1)} %get-tuple-element.189), channel_id=1, source_target_pairs={{0,16},{4,20},{8,24},{1,17},{5,21},{9,25},{2,18},{6,22},{10,26},{3... | collective-permute-start | bytes 1179656 | tf_op jit(solution)/shard_map/ppermute | solution.py:91
  919.6 18.0 %collective-permute-start.11 = (bf16[128,1536]{1,0:T(8,128)(2,1)S(1)}, bf16[128,1536]{1,0:T(8,128)(2,1)S(1)}, u32[]{:S(2)}, u32[]{:S(2)}) collective-permute-start(bf16[128,1536]{1,0:T(8,128)(2,1)S(1)} %get-tuple-element.188), channel_id=1, source_target_pairs={{0,20},{4,24},{28,16},{1,21},{5,25},{29,17},{2,22},{6,26},{30,18},... | collective-permute-start | bytes 1179656 | tf_op jit(solution)/shard_map/ppermute | solution.py:91
  921.6 22.7 %collective-permute-start.12 = (bf16[128,1536]{1,0:T(8,128)(2,1)S(1)}, bf16[128,1536]{1,0:T(8,128)(2,1)S(1)}, u32[]{:S(2)}, u32[]{:S(2)}) collective-permute-start(bf16[128,1536]{1,0:T(8,128)(2,1)S(1)} %get-tuple-element.187), channel_id=1, source_target_pairs={{0,24},{24,16},{28,20},{1,25},{25,17},{29,21},{2,26},{26,18},{30,2... | collective-permute-start | bytes 1179656 | tf_op jit(solution)/shard_map/ppermute | solution.py:91
  928.8 16.3 collective-permute-start.13
  945.9 270.9 %all-gather.31.cloned.1.call-start = ((), (), s32[]{:S(2)}) async-start(), calls=%async_computation.25 | async-start | bytes 15728640 | tf_op jit(solution)/shard_map/all_gather | solution.py:411
  951.5 52.4 %collective-permute-start = (bf16[128,1536]{0,1:T(8,128)(2,1)S(1)}, bf16[128,1536]{0,1:T(8,128)(2,1)S(1)}, u32[]{:S(2)}, u32[]{:S(2)}) collective-permute-start(bf16[128,1536]{0,1:T(8,128)(2,1)S(1)} %get-tuple-element.200), channel_id=1, source_target_pairs={{12,16},{16,20},{20,24},{13,17},{17,21},{21,25},{14,18},{18,22},{2... | collective-permute-start | bytes 1179656 | tf_op jit(solution)/shard_map/ppermute | solution.py:91
  952.2 56.8 %collective-permute-start.1 = (bf16[128,1536]{0,1:T(8,128)(2,1)S(1)}, bf16[128,1536]{0,1:T(8,128)(2,1)S(1)}, u32[]{:S(2)}, u32[]{:S(2)}) collective-permute-start(bf16[128,1536]{0,1:T(8,128)(2,1)S(1)} %get-tuple-element.199), channel_id=1, source_target_pairs={{8,16},{12,20},{16,24},{9,17},{13,21},{17,25},{10,18},{14,22},{18,... | collective-permute-start | bytes 1179656 | tf_op jit(solution)/shard_map/ppermute | solution.py:91
  952.9 57.6 %collective-permute-start.2 = (bf16[128,1536]{0,1:T(8,128)(2,1)S(1)}, bf16[128,1536]{0,1:T(8,128)(2,1)S(1)}, u32[]{:S(2)}, u32[]{:S(2)}) collective-permute-start(bf16[128,1536]{0,1:T(8,128)(2,1)S(1)} %get-tuple-element.198), channel_id=1, source_target_pairs={{4,16},{8,20},{12,24},{5,17},{9,21},{13,25},{6,18},{10,22},{14,26}... | collective-permute-start | bytes 1179656 | tf_op jit(solution)/shard_map/ppermute | solution.py:91
  953.6 58.2 %collective-permute-start.3 = (bf16[128,1536]{0,1:T(8,128)(2,1)S(1)}, bf16[128,1536]{0,1:T(8,128)(2,1)S(1)}, u32[]{:S(2)}, u32[]{:S(2)}) collective-permute-start(bf16[128,1536]{0,1:T(8,128)(2,1)S(1)} %get-tuple-element.197), channel_id=1, source_target_pairs={{0,16},{4,20},{8,24},{1,17},{5,21},{9,25},{2,18},{6,22},{10,26},{3... | collective-permute-start | bytes 1179656 | tf_op jit(solution)/shard_map/ppermute | solution.py:91
  1002.3 18.0 %collective-permute-start.4 = (bf16[128,1536]{0,1:T(8,128)(2,1)S(1)}, bf16[128,1536]{0,1:T(8,128)(2,1)S(1)}, u32[]{:S(2)}, u32[]{:S(2)}) collective-permute-start(bf16[128,1536]{0,1:T(8,128)(2,1)S(1)} %get-tuple-element.196), channel_id=1, source_target_pairs={{0,20},{4,24},{28,16},{1,21},{5,25},{29,17},{2,22},{6,26},{30,18},... | collective-permute-start | bytes 1179656 | tf_op jit(solution)/shard_map/ppermute | solution.py:91
  1004.0 21.1 %collective-permute-start.5 = (bf16[128,1536]{0,1:T(8,128)(2,1)S(1)}, bf16[128,1536]{0,1:T(8,128)(2,1)S(1)}, u32[]{:S(2)}, u32[]{:S(2)}) collective-permute-start(bf16[128,1536]{0,1:T(8,128)(2,1)S(1)} %get-tuple-element.195), channel_id=1, source_target_pairs={{0,24},{24,16},{28,20},{1,25},{25,17},{29,21},{2,26},{26,18},{30,2... | collective-permute-start | bytes 1179656 | tf_op jit(solution)/shard_map/ppermute | solution.py:91
  1009.0 16.9 %collective-permute-start.6 = (bf16[128,1536]{0,1:T(8,128)(2,1)S(1)}, bf16[128,1536]{0,1:T(8,128)(2,1)S(1)}, u32[]{:S(2)}, u32[]{:S(2)}) collective-permute-start(bf16[128,1536]{0,1:T(8,128)(2,1)S(1)} %get-tuple-element.194), channel_id=1, source_target_pairs={{20,16},{24,20},{28,24},{21,17},{25,21},{29,25},{22,18},{26,22},{3... | collective-permute-start | bytes 1179656 | tf_op jit(solution)/shard_map/ppermute | solution.py:91
  1031.5 84.0 %copy-start.12 = (bf16[128,1536]{1,0:T(8,128)(2,1)S(1)}, bf16[128,1536]{1,0:T(8,128)(2,1)}, u32[]{:S(2)}) copy-start(bf16[128,1536]{1,0:T(8,128)(2,1)} %reduce-scatter.10.cloned.1.call-done) | copy-start | bytes 1179652
  1031.5 84.0 %copy-start.14 = (bf16[1,128,1536]{2,1,0:T(8,128)(2,1)S(1)}, bf16[1,128,1536]{2,1,0:T(8,128)(2,1)}, u32[]{:S(2)}) copy-start(bf16[1,128,1536]{2,1,0:T(8,128)(2,1)} %param.25) | copy-start | bytes 1179652
  1031.5 84.0 %copy-start.38 = (f32[1536]{0:T(1024)S(1)}, f32[1536]{0:T(1024)}, u32[]{:S(2)}) copy-start(f32[1536]{0:T(1024)} %copy-done.37) | copy-start | bytes 18436
  1033.2 82.4 %copy-start.51 = (f32[128]{0:T(128)S(1)}, f32[128]{0:T(128)}, u32[]{:S(2)}) copy-start(f32[128]{0:T(128)} %add_rsqrt_fusion.3) | copy-start | bytes 1540
  1033.2 82.4 %copy-start.57 = (f32[128]{0:T(128)S(1)}, f32[128]{0:T(128)}, u32[]{:S(2)}) copy-start(f32[128]{0:T(128)} %copy-done.56) | copy-start | bytes 1540
  1300.9 31.8 %slice-start = ((s8[9437184]{0:T(1024)(128)(4,1)}), s8[1048576]{0:T(1024)(128)(4,1)S(1)}, s32[]{:S(2)}) async-start(s8[9437184]{0:T(1024)(128)(4,1)} %bitcast.324), calls=%async_computation.31 | async-start | bytes 2097152
  1300.9 31.8 %slice-start.1 = ((s8[9437184]{0:T(1024)(128)(4,1)}), s8[4194304]{0:T(1024)(128)(4,1)S(1)}, s32[]{:S(2)}) async-start(s8[9437184]{0:T(1024)(128)(4,1)} %bitcast.324), calls=%async_computation.32 | async-start | bytes 8388608
  1535.2 123.6 %all-to-all-start.4 = ((bf16[8,48,1536]{2,1,0:T(8,128)(2,1)}), bf16[8,48,1536]{2,1,0:T(8,128)(2,1)}, u32[]{:S(2)}, u32[]{:S(2)}) async-start(bf16[8,48,1536]{2,1,0:T(8,128)(2,1)} %bitcast.313), calls=%async_computation.10 | async-start | bytes 2359296 | tf_op jit(solution)/shard_map/all_to_all | solution.py:112
  1556.9 98.0 %copy-start.7 = (f32[2,1536,128]{1,2,0:T(8,128)S(1)}, f32[2,1536,128]{1,2,0:T(8,128)}, u32[]{:S(2)}) copy-start(f32[2,1536,128]{1,2,0:T(8,128)} %copy.130) | copy-start | bytes 4718596
  1557.0 4.9 collective-permute-start.14
  1557.8 5.4 collective-permute-start.15
  1558.5 5.4 collective-permute-start.16
  1559.2 93.9 %collective-permute-start.17 = (bf16[128,1536]{1,0:T(8,128)(2,1)S(1)}, bf16[128,1536]{1,0:T(8,128)(2,1)S(1)}, u32[]{:S(2)}, u32[]{:S(2)}) collective-permute-start(bf16[128,1536]{1,0:T(8,128)(2,1)S(1)} %get-tuple-element.180), channel_id=1, source_target_pairs={{16,0},{20,4},{24,8},{17,1},{21,5},{25,9},{18,2},{22,6},{26,10},{1... | collective-permute-start | bytes 1179656 | tf_op jit(solution)/shard_map/ppermute | solution.py:102
  1560.5 92.7 %collective-permute-start.18 = (bf16[128,1536]{1,0:T(8,128)(2,1)S(1)}, bf16[128,1536]{1,0:T(8,128)(2,1)S(1)}, u32[]{:S(2)}, u32[]{:S(2)}) collective-permute-start(bf16[128,1536]{1,0:T(8,128)(2,1)S(1)} %get-tuple-element.179), channel_id=1, source_target_pairs={{16,28},{20,0},{24,4},{17,29},{21,1},{25,5},{18,30},{22,2},{26,6},... | collective-permute-start | bytes 1179656 | tf_op jit(solution)/shard_map/ppermute | solution.py:102
  1561.8 91.4 %collective-permute-start.19 = (bf16[128,1536]{1,0:T(8,128)(2,1)S(1)}, bf16[128,1536]{1,0:T(8,128)(2,1)S(1)}, u32[]{:S(2)}, u32[]{:S(2)}) collective-permute-start(bf16[128,1536]{1,0:T(8,128)(2,1)S(1)} %get-tuple-element.178), channel_id=1, source_target_pairs={{16,24},{20,28},{24,0},{17,25},{21,29},{25,1},{18,26},{22,30},{26,... | collective-permute-start | bytes 1179656 | tf_op jit(solution)/shard_map/ppermute | solution.py:102
  1563.2 90.1 %collective-permute-start.20 = (bf16[128,1536]{1,0:T(8,128)(2,1)S(1)}, bf16[128,1536]{1,0:T(8,128)(2,1)S(1)}, u32[]{:S(2)}, u32[]{:S(2)}) collective-permute-start(bf16[128,1536]{1,0:T(8,128)(2,1)S(1)} %get-tuple-element.177), channel_id=1, source_target_pairs={{16,20},{20,24},{24,28},{17,21},{21,25},{25,29},{18,22},{22,26},{2... | collective-permute-start | bytes 1179656 | tf_op jit(solution)/shard_map/ppermute | solution.py:102
  (59 other events, 484.6 us)
Sparse Core Ops, SparseCore 0:
  33.8 22.4 all-gather.36
  58.5 60.4 all-gather.34
  121.2 18.3 all-gather.22
  141.5 60.4 all-gather.38
  205.3 62.2 all-gather.18
  270.2 59.2 all-gather.16
  331.7 27.5 all-gather.20
  373.9 74.3 reduce-scatter.9
  453.4 59.5 all-gather.24
  539.0 79.8 all-reduce.6
  621.5 38.0 reduce-scatter.17
  662.1 58.3 reduce-scatter.15
  723.7 25.7 reduce-scatter.13
  753.3 94.3 reduce-scatter.11
  851.5 117.6 reduce-scatter.7
  970.7 39.6 all-gather.26
  1011.9 37.4 all-gather.28
  1050.9 82.0 all-gather.32
  1134.6 82.0 all-gather.30
